TPU v7x, 32 devices: a whole 2x2x4 slice. The times are simulated.
32 devices in a mesh: grp: 2 (over x), seq: 16 (over z, y, core).
Axes of the slice: x: 2, y: 2, z: 4, core: 2. Of those that a mesh axis runs over, the one named last changes fastest.
Arguments:
- corpus: bfloat16 [8192, 3584], P(('grp', 'seq')), parts along dimension 0, may hold values from -6 to 6
- window_ends: int32 [64], P(('grp', 'seq')), parts along dimension 0, may hold values from 0 to 255
- norm_gain: float32 [3584], replicated, may hold values from 0.5 to 1.5
- routes: int32 [1024, 2], P(('grp', 'seq')), parts along dimension 0, may hold values from 0 to 15, all different within a row; in each aligned block of 32 rows (0 to 31, 32 to 63, ...) at most 8 rows name the same one
- in_blocks: int32 [16, 7], replicated, may hold values from 0 to 27, all different within a row
- out_blocks: int32 [16, 7], replicated, may hold values from 0 to 27, all different within a row
- enc_weight: bfloat16 [896, 32768], P(None, 'seq'), may hold values from -0.1875 to 0.1875
- enc_bias: float32 [32768], P('seq'), may hold values from -3 to 3
- latent_cutoffs: float32 [32768], P('seq'), may hold values from 0.2 to 1.2
- dec_weight: bfloat16 [32768, 896], P('seq'), may hold values from -0.125 to 0.125
- readout: float32 [32768], P('seq'), may hold values from -1.5 to 1.5
- dec_bias: float32 [3584], replicated, may hold values from -3 to 3
Outputs:
- reconstruction: bfloat16 [8192, 3584], P(('grp', 'seq')), parts along dimension 0
- attribution: bfloat16 [8192, 3584], P(('grp', 'seq')), parts along dimension 0
- feature_score: float32 [8192], P(('grp', 'seq')), parts along dimension 0
There are 2 independent parts, one for each index of `grp`. A program takes and returns all parts, laid end to end along the dimension named above; an argument that names none is the same for every part. Nothing has to cross between parts.
Inputs may be any that keep to these rules, and one draw needn't show every extreme that they name: `routes`: each segment names 2 different feature groups; within the 32 segments of one device no group is named more than 8 times. `in_blocks`: each row names 7 different blocks, and every block is named by some row. `out_blocks`: each row names 7 different blocks, and every block is named by some row.
All inputs are finite; a program needn't handle non-finite values.
Results may differ from a plain program's by a relative error of at most 0.012.
Values may be sent and summed in bfloat16 or wider, within the bound.
No kernel may reach another device: no remote copies, remote signals or barrier semaphores. Data moves between devices by JAX's collectives and lax.ppermute only.
A program may use at most 128 MiB of HBM per device.

v0:
```python
import functools

import jax
import jax.numpy as jnp
from jax import lax
from jax.experimental import pallas as pl
from jax.experimental.pallas import tpu as pltpu
from jax.sharding import PartitionSpec as P


BLK = 128
KEEP = 7
LEN = 128
SEG = 8
step_sharpness = 0.1
norm_eps = 1e-06
PIECES = 4


SMEM = pl.BlockSpec(memory_space=pltpu.SMEM)
VMEM = pl.BlockSpec(memory_space=pltpu.VMEM)
ANY = pl.BlockSpec(memory_space=pl.ANY)


def send_order(groups):
    quarter = groups // 4
    return [s for part in (2, 1, 3, 0) for s in range(part * quarter, (part + 1) * quarter)]


def clear_counts(counts, groups):
    def zero(i, carry):
        counts[i] = 0
        return carry

    lax.fori_loop(0, groups, zero, 0)


def normalize_rows(x, gain, width):
    x = x.astype(jnp.float32)
    mean = jnp.sum(x * x, axis=1, keepdims=True) * (1.0 / width)
    return (x * lax.rsqrt(mean + norm_eps) * gain).astype(jnp.bfloat16).astype(jnp.float32)


def own_kernel(gain_ref, corpus_ref, own_ref):
    rows, width = corpus_ref.shape
    gain = gain_ref[...]

    def body(i, carry):
        at = pl.ds(pl.multiple_of(i * 16, 16), 16)
        own_ref[at, :] = normalize_rows(corpus_ref[at, :], gain, width)
        return carry

    lax.fori_loop(0, rows // 16, body, 0)


def place_items(t, fanout, lowest, members, me, routes_ref, in_ref, counts, normal_ref, stage):
    for k in range(fanout):
        group = routes_ref[t * fanout + k]
        slot = counts[group]
        counts[group] = slot + 1
        partner = (group ^ me) - lowest

        @pl.when(jnp.logical_and(partner >= 0, partner < members))
        def _():
            for q in range(KEEP):
                at = pl.multiple_of(in_ref[group * KEEP + q] * BLK, BLK)
                stage[partner, q, slot] = normal_ref[t, :, pl.ds(at, BLK)]


def send_stage(stage, outs, sems):
    copies = [
        pltpu.make_async_copy(stage.at[s], out, sems.at[s]) for s, out in enumerate(outs)
    ]
    for copy in copies:
        copy.start()
    for copy in copies:
        copy.wait()


def far_kernel(groups, fanout, windows, *refs):
    members = groups // 2
    me_ref, ends_ref, routes_ref, in_ref, gain_ref, own_ref, below_ref = refs[:7]
    normal_ref = refs[7]
    outs = refs[8 : 8 + members]
    ext, stage, counts, sems = refs[8 + members :]
    width = own_ref.shape[1]
    gain = gain_ref[...]

    def body(i, carry):
        at = pl.ds(pl.multiple_of(i * 16, 16), 16)
        ext[at, :] = normalize_rows(below_ref[at, :], gain, width)
        return carry

    lowest = ends_ref[0] + 1
    for w in range(1, windows):
        lowest = jnp.minimum(lowest, ends_ref[w] + 1)
    lax.fori_loop(jnp.minimum(lowest, LEN) // 16, LEN // 16, body, 0)
    ext[LEN:, :] = own_ref[:SEG, :]
    clear_counts(counts, groups)
    me = me_ref[0]
    segs_per_window = LEN // SEG
    last = own_ref.shape[0] - SEG
    sublane = lax.broadcasted_iota(jnp.int32, (SEG, width), 0)
    for w in range(windows):
        first = ends_ref[w] + 1
        offset = lax.rem(first, SEG)
        base = first - offset
        turn = lax.rem(SEG - offset, SEG)

        def take(j, low_rows, high_rows):
            t = w * segs_per_window + j
            rows = jnp.where(
                sublane < SEG - offset,
                pltpu.roll(low_rows, turn, 0),
                pltpu.roll(high_rows, turn, 0),
            )
            normal_ref[t] = rows.astype(jnp.bfloat16)
            place_items(
                t, fanout, groups - members, members, me, routes_ref, in_ref, counts,
                normal_ref, stage,
            )

        def from_below(j, carry):
            low = pl.multiple_of(base + j * SEG, SEG)
            take(j, ext[pl.ds(low, SEG), :], ext[pl.ds(low + SEG, SEG), :])
            return carry

        def from_own(j, carry):
            low = pl.multiple_of(base + j * SEG - LEN, SEG)
            high = pl.multiple_of(jnp.minimum(low + SEG, last), SEG)
            take(j, own_ref[pl.ds(low, SEG), :], own_ref[pl.ds(high, SEG), :])
            return carry

        split = jnp.clip((LEN - base) // SEG, 0, segs_per_window)
        lax.fori_loop(0, split, from_below, 0)
        lax.fori_loop(split, segs_per_window, from_own, 0)
    send_stage(stage, outs, sems)


def near_kernel(groups, fanout, *refs):
    members = groups // 2
    me_ref, routes_ref, in_ref, normal_ref = refs[:4]
    outs = refs[4 : 4 + members]
    stage, counts, sems = refs[4 + members :]
    clear_counts(counts, groups)
    me = me_ref[0]

    def body(t, carry):
        place_items(
            t, fanout, 0, members, me, routes_ref, in_ref, counts, normal_ref, stage
        )
        return carry

    lax.fori_loop(0, normal_ref.shape[0], body, 0)
    send_stage(stage, outs, sems)


def features_kernel(count, cap, *refs):
    xs = refs[:count]
    enc_ref, dec_ref, bias_ref, cut_ref, read_ref = refs[count : count + 5]
    outs = refs[count + 6 : 2 * count + 6]
    x_all, dec_acc, pull_acc, score_acc = refs[2 * count + 6 :]
    step = pl.program_id(0)
    rows = cap * SEG

    @pl.when(step == 0)
    def _():
        for i in range(count):
            for q in range(KEEP):
                x_all[i * rows : (i + 1) * rows, q * BLK : (q + 1) * BLK] = xs[i][q]
        dec_acc[...] = jnp.zeros_like(dec_acc)
        pull_acc[...] = jnp.zeros_like(pull_acc)
        score_acc[...] = jnp.zeros_like(score_acc)

    pre = (
        jnp.dot(x_all[...], enc_ref[...], preferred_element_type=jnp.float32) + bias_ref[...]
    )
    readout = read_ref[...]
    firing = jax.nn.sigmoid((pre - cut_ref[...]) * (1.0 / step_sharpness))
    active = pre * firing
    slope = (
        readout * (firing + active * (1.0 - firing) * (1.0 / step_sharpness))
    ).astype(jnp.bfloat16)
    dec_acc[...] += jnp.dot(
        active.astype(jnp.bfloat16), dec_ref[...], preferred_element_type=jnp.float32
    )
    pull_acc[...] += lax.dot_general(
        slope, enc_ref[...], (((1,), (1,)), ((), ())), preferred_element_type=jnp.float32
    )
    weighted = readout * active
    part = weighted[:, :BLK]
    for j in range(1, weighted.shape[1] // BLK):
        part = part + weighted[:, j * BLK : (j + 1) * BLK]
    score_acc[...] += part

    @pl.when(step == pl.num_programs(0) - 1)
    def _():
        lanes = lax.broadcasted_iota(jnp.int32, (SEG, BLK), 1)
        totals = jnp.sum(score_acc[...], axis=1, keepdims=True)
        for i in range(count):
            for q in range(KEEP):
                for acc, base in ((dec_acc, 0), (pull_acc, KEEP)):
                    tile = acc[i * rows : (i + 1) * rows, q * BLK : (q + 1) * BLK]
                    outs[i][(base + q) * cap : (base + q + 1) * cap] = tile.astype(
                        jnp.bfloat16
                    ).reshape(cap, SEG, BLK)
            marks = jnp.zeros((SEG, BLK), jnp.float32)
            for c in range(cap):
                at = i * rows + c * SEG
                marks = jnp.where(lanes == c, totals[at : at + SEG], marks)
            outs[i][2 * KEEP * cap] = marks.astype(jnp.bfloat16)


def combine_kernel(groups, cap, fanout, segments, final, *refs):
    members = groups // 4 if final else groups - groups // 4
    me_ref, routes_ref, in_ref, out_ref = refs[:4]
    backs = refs[4 : 4 + members]
    if final:
        recon_acc, grad_acc, marks_acc, normal_ref = refs[4 + members : 8 + members]
        recon_out, attr_out, score_ref = refs[8 + members : 11 + members]
        stage, recon_ref, attr_ref, out_sems, counts, sems = refs[14 + members :]
    else:
        bias_ref = refs[4 + members]
        recon_acc, grad_acc, score_ref = refs[5 + members : 8 + members]
        stage, counts, sems = refs[8 + members :]
    copies = [
        pltpu.make_async_copy(backs[s], stage.at[s], sems.at[s]) for s in range(members)
    ]
    for copy in copies:
        copy.start()
    clear_counts(counts, groups)
    me = me_ref[0]
    lowest = groups - members if final else 0
    for copy in copies:
        copy.wait()
    lane = lax.broadcasted_iota(jnp.int32, (SEG, BLK), 1)
    sublane = lax.broadcasted_iota(jnp.int32, (SEG, BLK), 0)
    per_row = BLK // SEG
    if not final:
        bias = jnp.broadcast_to(bias_ref[...], recon_acc.shape[1:])

    def one(t, carry):
        if not final:
            recon_acc[t] = bias
            grad_acc[t] = jnp.zeros_like(bias)
            score_ref[t] = jnp.zeros((SEG, BLK), jnp.float32)
        for k in range(fanout):
            group = routes_ref[t * fanout + k]
            slot = counts[group]
            counts[group] = slot + 1
            partner = (group ^ me) - lowest
            here = jnp.logical_and(partner >= 0, partner < members)

            @pl.when(here)
            def _():
                for q in range(KEEP):
                    at = pl.ds(pl.multiple_of(out_ref[group * KEEP + q] * BLK, BLK), BLK)
                    recon_acc[t, :, at] += stage[partner, q * cap + slot].astype(jnp.float32)
                    at = pl.ds(pl.multiple_of(in_ref[group * KEEP + q] * BLK, BLK), BLK)
                    grad_acc[t, :, at] += stage[partner, (KEEP + q) * cap + slot].astype(
                        jnp.float32
                    )
                marks = stage[partner, 2 * KEEP * cap].astype(jnp.float32)
                held = marks_acc if final else score_ref
                held[t] += jnp.where(lane == slot, marks, 0.0)

        if final:
            recon_ref[t] = recon_acc[t].astype(jnp.bfloat16)
            attr_ref[t] = (normal_ref[t].astype(jnp.float32) * grad_acc[t]).astype(
                jnp.bfloat16
            )
        return carry

    if not final:
        lax.fori_loop(0, segments, one, 0)
    else:
        step = segments // PIECES
        leaving = []
        for piece in range(PIECES):
            lax.fori_loop(piece * step, (piece + 1) * step, one, 0)
            at = pl.ds(piece * step, step)
            for i, (held, out) in enumerate(((recon_ref, recon_out), (attr_ref, attr_out))):
                leaving.append(
                    pltpu.make_async_copy(held.at[at], out.at[at], out_sems.at[i, piece])
                )
                leaving[-1].start()
        for row in range(segments // per_row):
            line = jnp.zeros((SEG, BLK), jnp.float32)
            for i in range(per_row):
                total = jnp.sum(marks_acc[row * per_row + i], axis=1, keepdims=True)
                line = jnp.where(lane == i * SEG + sublane, total, line)
            score_ref[row : row + 1, :] = jnp.sum(line, axis=0, keepdims=True)
        for copy in leaving:
            copy.wait()


def program(
    corpus,
    window_ends,
    norm_gain,
    routes,
    in_blocks,
    out_blocks,
    enc_weight,
    enc_bias,
    latent_cutoffs,
    dec_weight,
    readout,
    dec_bias,
):
    groups = lax.axis_size("seq")
    width = corpus.shape[1]
    windows = window_ends.shape[0]
    segments, fanout = routes.shape
    features = enc_weight.shape[1]
    cap = max(2, 2 * segments * fanout // groups)
    me = lax.axis_index("seq").astype(jnp.int32).reshape(1)
    below = lax.ppermute(corpus[-LEN:], "seq", [(i, i + 1) for i in range(groups - 1)])
    flat_routes = routes.reshape(-1)
    flat_in = in_blocks.reshape(-1)
    flat_out = out_blocks.reshape(-1)

    own = pl.pallas_call(
        own_kernel,
        out_shape=jax.ShapeDtypeStruct(corpus.shape, jnp.float32),
        in_specs=[VMEM] * 2,
        out_specs=VMEM,
        cost_estimate=pl.CostEstimate(
            flops=6 * corpus.size, bytes_accessed=6 * corpus.size, transcendentals=0
        ),
        compiler_params=pltpu.CompilerParams(vmem_limit_bytes=12 << 20),
        name="own",
    )(norm_gain.reshape(1, -1), corpus)
    half = groups // 2
    slots = jax.ShapeDtypeStruct((KEEP, cap, SEG, BLK), jnp.bfloat16)
    pack_scratch = [
        pltpu.VMEM((half, KEEP, cap, SEG, BLK), jnp.bfloat16),
        pltpu.SMEM((groups,), jnp.int32),
        pltpu.SemaphoreType.DMA((half,)),
    ]
    far = pl.pallas_call(
        functools.partial(far_kernel, groups, fanout, windows),
        out_shape=(jax.ShapeDtypeStruct((segments, SEG, width), jnp.bfloat16),)
        + (slots,) * half,
        in_specs=[SMEM] * 4 + [VMEM] * 3,
        out_specs=(VMEM,) + (ANY,) * half,
        scratch_shapes=[pltpu.VMEM((LEN + SEG, width), jnp.float32)] + pack_scratch,
        cost_estimate=pl.CostEstimate(flops=10_000_000, bytes_accessed=8_000_000, transcendentals=0),
        compiler_params=pltpu.CompilerParams(vmem_limit_bytes=16 << 20),
        name="far",
    )(me, window_ends, flat_routes, flat_in, norm_gain.reshape(1, -1), own, below)
    normal = far[0]
    near = pl.pallas_call(
        functools.partial(near_kernel, groups, fanout),
        out_shape=(slots,) * half,
        in_specs=[SMEM] * 3 + [VMEM],
        out_specs=(ANY,) * half,
        scratch_shapes=pack_scratch,
        cost_estimate=pl.CostEstimate(
            flops=10_000_000, bytes_accessed=4_000_000, transcendentals=0
        ),
        compiler_params=pltpu.CompilerParams(vmem_limit_bytes=8 << 20),
        name="near",
    )(me, flat_routes, flat_in, normal)
    outgoing = tuple(near) + tuple(far[1:])

    def exchange(block, pattern):
        if pattern == 0:
            return block
        return lax.ppermute(block, "seq", [(i, i ^ pattern) for i in range(groups)])

    quarter = groups // 4
    arrived = {}
    for s in send_order(groups):
        arrived[s] = exchange(outgoing[s], s)

    rows = cap * SEG
    tile = 512
    features_call = pl.pallas_call(
        functools.partial(features_kernel, quarter, cap),
        grid=(features // tile,),
        out_shape=(
            jax.ShapeDtypeStruct((2 * KEEP * cap + 1, SEG, BLK), jnp.bfloat16),
        )
        * quarter,
        in_specs=[pl.BlockSpec((KEEP, rows, BLK), lambda f: (0, 0, 0))] * quarter
        + [
            pl.BlockSpec((KEEP * BLK, tile), lambda f: (0, f)),
            pl.BlockSpec((tile, KEEP * BLK), lambda f: (f, 0)),
            pl.BlockSpec((1, tile), lambda f: (0, f)),
            pl.BlockSpec((1, tile), lambda f: (0, f)),
            pl.BlockSpec((1, tile), lambda f: (0, f)),
            ANY,
        ],
        out_specs=(
            pl.BlockSpec((2 * KEEP * cap + 1, SEG, BLK), lambda f: (0, 0, 0)),
        )
        * quarter,
        scratch_shapes=[
            pltpu.VMEM((quarter * rows, KEEP * BLK), jnp.bfloat16),
            pltpu.VMEM((quarter * rows, KEEP * BLK), jnp.float32),
            pltpu.VMEM((quarter * rows, KEEP * BLK), jnp.float32),
            pltpu.VMEM((quarter * rows, BLK), jnp.float32),
        ],
        cost_estimate=pl.CostEstimate(
            flops=6 * quarter * rows * KEEP * BLK * features,
            bytes_accessed=4 * KEEP * BLK * features,
            transcendentals=quarter * rows * features,
        ),
        compiler_params=pltpu.CompilerParams(vmem_limit_bytes=20 << 20),
        name="features",
    )
    returned = {}
    turn = me
    for part in [1, 2, 0, 3]:
        members = list(range(part * quarter, (part + 1) * quarter))
        results = features_call(
            *[arrived[s].reshape(KEEP, rows, BLK) for s in members],
            enc_weight,
            dec_weight,
            enc_bias.reshape(1, -1),
            latent_cutoffs.reshape(1, -1),
            readout.reshape(1, -1),
            turn,
        )
        turn = results[0]
        for s, result in zip(members, results):
            returned[s] = exchange(result, s)

    def combine(final, members, out_shape, in_specs, out_specs, scratch, aliases, *rest):
        return pl.pallas_call(
            functools.partial(combine_kernel, groups, cap, fanout, segments, final),
            out_shape=out_shape,
            in_specs=[SMEM] * 4 + [ANY] * len(members) + in_specs,
            out_specs=out_specs,
            input_output_aliases=aliases,
            scratch_shapes=[
                pltpu.VMEM((len(members), 2 * KEEP * cap + 1, SEG, BLK), jnp.bfloat16),
                *scratch,
                pltpu.SMEM((groups,), jnp.int32),
                pltpu.SemaphoreType.DMA((len(members),)),
            ],
            cost_estimate=pl.CostEstimate(
                flops=10_000_000, bytes_accessed=10_000_000, transcendentals=0
            ),
            compiler_params=pltpu.CompilerParams(vmem_limit_bytes=20 << 20),
            name="combine",
        )(
            me,
            flat_routes,
            flat_in,
            flat_out,
            *[returned[s] for s in members],
            *rest,
        )

    wide = jax.ShapeDtypeStruct((segments, SEG, width), jnp.float32)
    thin = jax.ShapeDtypeStruct((segments, SEG, width), jnp.bfloat16)
    marks = jax.ShapeDtypeStruct((segments, SEG, BLK), jnp.float32)
    parts = combine(
        False,
        range(groups - quarter),
        (wide, wide, marks),
        [VMEM],
        (VMEM,) * 3,
        [],
        {},
        dec_bias.reshape(1, -1),
    )
    first = 4 + quarter
    recon, attr, score = combine(
        True,
        range(groups - quarter, groups),
        (thin, thin, jax.ShapeDtypeStruct((segments * SEG // BLK, BLK), jnp.float32))
        + (wide, wide, marks),
        [VMEM] * 4,
        (ANY, ANY, VMEM) + (ANY,) * 3,
        [pltpu.VMEM((segments, SEG, width), jnp.bfloat16)] * 2
        + [pltpu.SemaphoreType.DMA((2, PIECES))],
        {first: 3, first + 1: 4, first + 2: 5},
        *parts,
        normal,
    )[:3]
    feature_score = score.reshape(-1)
    return (recon.reshape(-1, width), attr.reshape(-1, width), feature_score)


def solution(mesh):
    in_specs = (
        P(("grp", "seq"), None),
        P(("grp", "seq")),
        P(),
        P(("grp", "seq"), None),
        P(),
        P(),
        P(None, "seq"),
        P("seq"),
        P("seq"),
        P("seq", None),
        P("seq"),
        P(),
    )
    out_specs = (P(("grp", "seq"), None), P(("grp", "seq"), None), P(("grp", "seq")))
    return jax.shard_map(
        program, mesh=mesh, in_specs=in_specs, out_specs=out_specs, check_vma=False
    )
```

profile of v0, /device:TPU:13, one launch (start us, length us, event | category | flops | bytes accessed | tf_op | source)
XLA Modules:
  0.0 167.4 jit_solution(12237100028022813440)
XLA Ops:
  1.9 3.7 %collective-permute-start = (bf16[128,3584]{1,0:T(8,128)(2,1)S(1)}, bf16[128,3584]{1,0:T(8,128)(2,1)S(1)}, u32[]{:S(2)}, u32[]{:S(2)}) collective-permute-start(bf16[128,3584]{1,0:T(8,128)(2,1)S(1)} %slice.3), channel_id=1, source_target_pairs={{0,1},{1,2},{2,3},{3,4},{4,5},{5,6},{6,7},{7,8},{8,9},{9,10},{10,1... | collective-permute-start | bytes 2752520 | tf_op jit(solution)/shard_map/ppermute | solution.py:318
  9.6 2.5 %own.1.refs_5_ = f32[256,3584]{1,0:T(8,128)S(1)} custom-call(f32[1,3584]{1,0:T(1,128)S(1)} %reshape.104.gain_ref.refs_4_, bf16[256,3584]{1,0:T(8,128)(2,1)S(1)} %copy-done), custom_call_target="tpu_custom_call" | custom-call | flops 5505024 | bytes 5505024 | tf_op jit(solution)/shard_map/own/pallas_call | solution.py:323
  12.1 3.8 %collective-permute-done.refs_6_ = bf16[128,3584]{1,0:T(8,128)(2,1)S(1)} collective-permute-done((bf16[128,3584]{1,0:T(8,128)(2,1)S(1)}, bf16[128,3584]{1,0:T(8,128)(2,1)S(1)}, u32[]{:S(2)}, u32[]{:S(2)}) %collective-permute-start) | collective-permute-done | bytes 917536 | tf_op jit(solution)/shard_map/ppermute | solution.py:318
  15.9 4.8 %far.1 = (bf16[32,8,3584]{2,1,0:T(8,128)(2,1)S(1)}, bf16[7,8,8,128]{3,2,1,0:T(8,128)(2,1)S(1)}, bf16[7,8,8,128]{3,2,1,0:T(8,128)(2,1)S(1)}, bf16[7,8,8,128]{3,2,...) custom-call(s32[1]{0:T(128)} %bitcast.refs_0_.refs_9_, ...), custom_call_target="tpu_custom_call" | custom-call | flops 10000000 | bytes 8000000 | tf_op jit(solution)/shard_map/far/pallas_call | solution.py:341
  21.4 1.8 %collective-permute-start.2 = (bf16[7,8,8,128]{3,2,1,0:T(8,128)(2,1)S(1)}, bf16[7,8,8,128]{3,2,1,0:T(8,128)(2,1)S(1)}, u32[]{:S(2)}, u32[]{:S(2)}) collective-permute-start(bf16[7,8,8,128]{3,2,1,0:T(8,128)(2,1)S(1)} %get-tuple-element.43), channel_id=1, source_target_pairs={{0,13},{1,12},{2,15},{3,14},{4,9},{5,8},{6,11},{7,10},{8,5},{9,4},... | collective-permute-start | bytes 344072 | tf_op jit(solution)/shard_map/ppermute | solution.py:370
  23.1 3.3 %near.1 = (bf16[7,8,8,128]{3,2,1,0:T(8,128)(2,1)S(1)}, bf16[7,8,8,128]{3,2,1,0:T(8,128)(2,1)S(1)}, bf16[7,8,8,128]{3,2,1,0:T(8,128)(2,1)S(1)}, bf16[7,8,8,128]{3...) custom-call(s32[1]{0:T(128)} %bitcast.refs_0_.refs_9_, ...), custom_call_target="tpu_custom_call" | custom-call | flops 10000000 | bytes 4000000 | tf_op jit(solution)/shard_map/near/pallas_call | solution.py:353
  26.4 2.7 %collective-permute-start.12 = (bf16[7,8,8,128]{3,2,1,0:T(8,128)(2,1)S(1)}, bf16[7,8,8,128]{3,2,1,0:T(8,128)(2,1)S(1)}, u32[]{:S(2)}, u32[]{:S(2)}) collective-permute-start(bf16[7,8,8,128]{3,2,1,0:T(8,128)(2,1)S(1)} %get-tuple-element.55), channel_id=1, source_target_pairs={{0,4},{1,5},{2,6},{3,7},{4,0},{5,1},{6,2},{7,3},{8,12},{9,13},{10,... | collective-permute-start | bytes 344072 | tf_op jit(solution)/shard_map/ppermute | solution.py:370
  29.2 2.2 %collective-permute-start.14 = (bf16[7,8,8,128]{3,2,1,0:T(8,128)(2,1)S(1)}, bf16[7,8,8,128]{3,2,1,0:T(8,128)(2,1)S(1)}, u32[]{:S(2)}, u32[]{:S(2)}) collective-permute-start(bf16[7,8,8,128]{3,2,1,0:T(8,128)(2,1)S(1)} %get-tuple-element.57), channel_id=1, source_target_pairs={{0,6},{1,7},{2,4},{3,5},{4,2},{5,3},{6,0},{7,1},{8,14},{9,15},{10,... | collective-permute-start | bytes 344072 | tf_op jit(solution)/shard_map/ppermute | solution.py:370
  33.4 1.8 %collective-permute-start.3 = (bf16[7,8,8,128]{3,2,1,0:T(8,128)(2,1)S(1)}, bf16[7,8,8,128]{3,2,1,0:T(8,128)(2,1)S(1)}, u32[]{:S(2)}, u32[]{:S(2)}) collective-permute-start(bf16[7,8,8,128]{3,2,1,0:T(8,128)(2,1)S(1)} %get-tuple-element.44), channel_id=1, source_target_pairs={{0,14},{1,15},{2,12},{3,13},{4,10},{5,11},{6,8},{7,9},{8,6},{9,7},... | collective-permute-start | bytes 344072 | tf_op jit(solution)/shard_map/ppermute | solution.py:370
  36.5 2.3 %collective-permute-start.9 = (bf16[7,8,8,128]{3,2,1,0:T(8,128)(2,1)S(1)}, bf16[7,8,8,128]{3,2,1,0:T(8,128)(2,1)S(1)}, u32[]{:S(2)}, u32[]{:S(2)}) collective-permute-start(bf16[7,8,8,128]{3,2,1,0:T(8,128)(2,1)S(1)} %get-tuple-element.52), channel_id=1, source_target_pairs={{0,9},{1,8},{2,11},{3,10},{4,13},{5,12},{6,15},{7,14},{8,1},{9,0},... | collective-permute-start | bytes 344072 | tf_op jit(solution)/shard_map/ppermute | solution.py:370
  38.8 2.7 %collective-permute-start.10 = (bf16[7,8,8,128]{3,2,1,0:T(8,128)(2,1)S(1)}, bf16[7,8,8,128]{3,2,1,0:T(8,128)(2,1)S(1)}, u32[]{:S(2)}, u32[]{:S(2)}) collective-permute-start(bf16[7,8,8,128]{3,2,1,0:T(8,128)(2,1)S(1)} %get-tuple-element.53), channel_id=1, source_target_pairs={{0,10},{1,11},{2,8},{3,9},{4,14},{5,15},{6,12},{7,13},{8,2},{9,3},... | collective-permute-start | bytes 344072 | tf_op jit(solution)/shard_map/ppermute | solution.py:370
  41.5 1.8 %collective-permute-done.15 = bf16[7,8,8,128]{3,2,1,0:T(8,128)(2,1)S(1)} collective-permute-done((bf16[7,8,8,128]{3,2,1,0:T(8,128)(2,1)S(1)}, bf16[7,8,8,128]{3,2,1,0:T(8,128)(2,1)S(1)}, u32[]{:S(2)}, u32[]{:S(2)}) %collective-permute-start.15) | collective-permute-done | bytes 114720 | tf_op jit(solution)/shard_map/ppermute | solution.py:370
  43.3 5.6 %collective-permute-start.11 = (bf16[7,8,8,128]{3,2,1,0:T(8,128)(2,1)S(1)}, bf16[7,8,8,128]{3,2,1,0:T(8,128)(2,1)S(1)}, u32[]{:S(2)}, u32[]{:S(2)}) collective-permute-start(bf16[7,8,8,128]{3,2,1,0:T(8,128)(2,1)S(1)} %get-tuple-element.54), channel_id=1, source_target_pairs={{0,11},{1,10},{2,9},{3,8},{4,15},{5,14},{6,13},{7,12},{8,3},{9,2},... | collective-permute-start | bytes 344072 | tf_op jit(solution)/shard_map/ppermute | solution.py:370
  49.0 5.7 %features.4 = (bf16[113,8,128]{2,1,0:T(8,128)(2,1)S(1)}, bf16[113,8,128]{2,1,0:T(8,128)(2,1)S(1)}, bf16[113,8,128]{2,1,0:T(8,128)(2,1)S(1)}, bf16[113,8,128]{2,1,0:T(8,128)(2,1)S(1)}) custom-call(bf16[7,64,128]{2,1,0:T(8,128)(2,1)S(1)} %bitcast.34, bf16[7,64,128]{2,1,0:T(8,128)(2,1)S(1)} %bitcast.35, bf16[7,64,128]{2,1,0:T(8,128)(2,1)S(1)} %bitcast.37, ...), custom_call_target="tpu_custom_call" | custom-call | flops 2818572288 | bytes 7340032 | tf_op jit(solution)/shard_map/features/pallas_call | solution.py:417
  56.3 3.2 %collective-permute-start.6 = (bf16[7,8,8,128]{3,2,1,0:T(8,128)(2,1)S(1)}, bf16[7,8,8,128]{3,2,1,0:T(8,128)(2,1)S(1)}, u32[]{:S(2)}, u32[]{:S(2)}) collective-permute-start(bf16[7,8,8,128]{3,2,1,0:T(8,128)(2,1)S(1)} %get-tuple-element.49), channel_id=1, source_target_pairs={{0,2},{1,3},{2,0},{3,1},{4,6},{5,7},{6,4},{7,5},{8,10},{9,11},{10,... | collective-permute-start | bytes 344072 | tf_op jit(solution)/shard_map/ppermute | solution.py:370
  59.5 1.8 %collective-permute-done.10 = bf16[7,8,8,128]{3,2,1,0:T(8,128)(2,1)S(1)} collective-permute-done((bf16[7,8,8,128]{3,2,1,0:T(8,128)(2,1)S(1)}, bf16[7,8,8,128]{3,2,1,0:T(8,128)(2,1)S(1)}, u32[]{:S(2)}, u32[]{:S(2)}) %collective-permute-start.10) | collective-permute-done | bytes 114720 | tf_op jit(solution)/shard_map/ppermute | solution.py:370
  63.7 3.2 %collective-permute-start.24 = (bf16[113,8,128]{2,1,0:T(8,128)(2,1)S(1)}, bf16[113,8,128]{2,1,0:T(8,128)(2,1)S(1)}, u32[]{:S(2)}, u32[]{:S(2)}) collective-permute-start(bf16[113,8,128]{2,1,0:T(8,128)(2,1)S(1)} %get-tuple-element.69), channel_id=1, source_target_pairs={{0,5},{1,4},{2,7},{3,6},{4,1},{5,0},{6,3},{7,2},{8,13},{9,12},{10,... | collective-permute-start | bytes 694280 | tf_op jit(solution)/shard_map/ppermute | solution.py:370
  66.9 5.7 %features.5 = (bf16[113,8,128]{2,1,0:T(8,128)(2,1)S(1)}, bf16[113,8,128]{2,1,0:T(8,128)(2,1)S(1)}, bf16[113,8,128]{2,1,0:T(8,128)(2,1)S(1)}, bf16[113,8,128]{2,1,0:T(8,128)(2,1)S(1)}) custom-call(bf16[7,64,128]{2,1,0:T(8,128)(2,1)S(1)} %bitcast.29, bf16[7,64,128]{2,1,0:T(8,128)(2,1)S(1)} %bitcast.31, bf16[7,64,128]{2,1,0:T(8,128)(2,1)S(1)} %bitcast.33, ...), custom_call_target="tpu_custom_call" | custom-call | flops 2818572288 | bytes 7340032 | tf_op jit(solution)/shard_map/features/pallas_call | solution.py:417
  72.7 1.6 collective-permute-start.25
  75.6 1.9 %collective-permute-start.28 = (bf16[113,8,128]{2,1,0:T(8,128)(2,1)S(1)}, bf16[113,8,128]{2,1,0:T(8,128)(2,1)S(1)}, u32[]{:S(2)}, u32[]{:S(2)}) collective-permute-start(bf16[113,8,128]{2,1,0:T(8,128)(2,1)S(1)} %get-tuple-element.72), channel_id=1, source_target_pairs={{0,9},{1,8},{2,11},{3,10},{4,13},{5,12},{6,15},{7,14},{8,1},{9,0},... | collective-permute-start | bytes 694280 | tf_op jit(solution)/shard_map/ppermute | solution.py:370
  78.4 6.4 %features.6 = (bf16[113,8,128]{2,1,0:T(8,128)(2,1)S(1)}, bf16[113,8,128]{2,1,0:T(8,128)(2,1)S(1)}, bf16[113,8,128]{2,1,0:T(8,128)(2,1)S(1)}, bf16[113,8,128]{2,1,0:T(8,128)(2,1)}) custom-call(bf16[7,64,128]{2,1,0:T(8,128)(2,1)S(1)} %bitcast.26, bf16[7,64,128]{2,1,0:T(8,128)(2,1)S(1)} %bitcast.28, bf16[7,64,128]{2,1,0:T(8,128)(2,1)S(1)} %bitcast.30, ...), custom_call_target="tpu_custom_call" | custom-call | flops 2818572288 | bytes 7340032 | tf_op jit(solution)/shard_map/features/pallas_call | solution.py:417
  84.7 7.7 %collective-permute-done.25.refs_10_ = bf16[113,8,128]{2,1,0:T(8,128)(2,1)S(1)} collective-permute-done((bf16[113,8,128]{2,1,0:T(8,128)(2,1)S(1)}, bf16[113,8,128]{2,1,0:T(8,128)(2,1)S(1)}, u32[]{:S(2)}, u32[]{:S(2)}) %collective-permute-start.25) | collective-permute-done | bytes 231456 | tf_op jit(solution)/shard_map/ppermute | solution.py:370
  92.5 3.4 %collective-permute-start.27 = (bf16[113,8,128]{2,1,0:T(8,128)(2,1)S(1)}, bf16[113,8,128]{2,1,0:T(8,128)(2,1)S(1)}, u32[]{:S(2)}, u32[]{:S(2)}) collective-permute-start(bf16[113,8,128]{2,1,0:T(8,128)(2,1)S(1)} %get-tuple-element.60.refs_9_), channel_id=1, source_target_pairs={{0,8},{1,9},{2,10},{3,11},{4,12},{5,13},{6,14},{7,15},{8,0},{9,1},... | collective-permute-start | bytes 694280 | tf_op jit(solution)/shard_map/ppermute | solution.py:370
  97.4 4.2 %collective-permute-start.30 = (bf16[113,8,128]{2,1,0:T(8,128)(2,1)S(1)}, bf16[113,8,128]{2,1,0:T(8,128)(2,1)S(1)}, u32[]{:S(2)}, u32[]{:S(2)}) collective-permute-start(bf16[113,8,128]{2,1,0:T(8,128)(2,1)S(1)} %get-tuple-element.74), channel_id=1, source_target_pairs={{0,11},{1,10},{2,9},{3,8},{4,15},{5,14},{6,13},{7,12},{8,3},{9,2},... | collective-permute-start | bytes 694280 | tf_op jit(solution)/shard_map/ppermute | solution.py:370
  103.7 6.6 %features.7 = (bf16[113,8,128]{2,1,0:T(8,128)(2,1)}, bf16[113,8,128]{2,1,0:T(8,128)(2,1)}, bf16[113,8,128]{2,1,0:T(8,128)(2,1)}, bf16[113,8,128]{2,1,0:T(8,128)(2,1)}) custom-call(bf16[7,64,128]{2,1,0:T(8,128)(2,1)S(1)} %bitcast.23, bf16[7,64,128]{2,1,0:T(8,128)(2,1)S(1)} %bitcast.24, bf16[7,64,128]{2,1,0:T(8,128)(2,1)S(1)} %bitcast.25, ...), custom_call_target="tpu_custom_call" | custom-call | flops 2818572288 | bytes 7340032 | tf_op jit(solution)/shard_map/features/pallas_call | solution.py:417
  110.3 8.6 %collective-permute-done.30.refs_15_ = bf16[113,8,128]{2,1,0:T(8,128)(2,1)S(1)} collective-permute-done((bf16[113,8,128]{2,1,0:T(8,128)(2,1)S(1)}, bf16[113,8,128]{2,1,0:T(8,128)(2,1)S(1)}, u32[]{:S(2)}, u32[]{:S(2)}) %collective-permute-start.30) | collective-permute-done | bytes 231456 | tf_op jit(solution)/shard_map/ppermute | solution.py:370
  133.8 6.7 %combine.2 = (f32[32,8,3584]{2,1,0:T(8,128)S(1)}, f32[32,8,3584]{2,1,0:T(8,128)S(1)}, f32[32,8,128]{2,1,0:T(8,128)S(1)}) custom-call(s32[1]{0:T(128)} %bitcast.refs_0_.refs_9_, s32[64]{0:T(128)S(1)} %reshape.101.refs_2_.refs_1_, s32[112]{0:T(128)S(1)} %reshape.102.refs_3_.refs_2_, s32[112]{0:T(128)S(1)} %reshape.103.refs_3_, ...), custom_call_target="tpu_custom_call" | custom-call | flops 10000000 | bytes 10000000 | tf_op jit(solution)/shard_map/combine/pallas_call | solution.py:431
  140.5 4.6 %collective-permute-done.16.refs_4_ = bf16[113,8,128]{2,1,0:T(8,128)(2,1)S(1)} collective-permute-done((bf16[113,8,128]{2,1,0:T(8,128)(2,1)}, bf16[113,8,128]{2,1,0:T(8,128)(2,1)S(1)}, u32[]{:S(2)}, u32[]{:S(2)}) %collective-permute-start.16) | collective-permute-done | bytes 231456 | tf_op jit(solution)/shard_map/ppermute | solution.py:370
  145.1 7.8 %collective-permute-done.17.refs_5_ = bf16[113,8,128]{2,1,0:T(8,128)(2,1)S(1)} collective-permute-done((bf16[113,8,128]{2,1,0:T(8,128)(2,1)}, bf16[113,8,128]{2,1,0:T(8,128)(2,1)S(1)}, u32[]{:S(2)}, u32[]{:S(2)}) %collective-permute-start.17) | collective-permute-done | bytes 231456 | tf_op jit(solution)/shard_map/ppermute | solution.py:370
  153.0 3.5 %collective-permute-done.18.refs_6_ = bf16[113,8,128]{2,1,0:T(8,128)(2,1)S(1)} collective-permute-done((bf16[113,8,128]{2,1,0:T(8,128)(2,1)}, bf16[113,8,128]{2,1,0:T(8,128)(2,1)S(1)}, u32[]{:S(2)}, u32[]{:S(2)}) %collective-permute-start.18) | collective-permute-done | bytes 231456 | tf_op jit(solution)/shard_map/ppermute | solution.py:370
  156.5 5.6 %collective-permute-done.19.refs_7_ = bf16[113,8,128]{2,1,0:T(8,128)(2,1)S(1)} collective-permute-done((bf16[113,8,128]{2,1,0:T(8,128)(2,1)}, bf16[113,8,128]{2,1,0:T(8,128)(2,1)S(1)}, u32[]{:S(2)}, u32[]{:S(2)}) %collective-permute-start.19) | collective-permute-done | bytes 231456 | tf_op jit(solution)/shard_map/ppermute | solution.py:370
  162.1 5.4 %combine.3 = (bf16[32,8,3584]{2,1,0:T(8,128)(2,1)}, bf16[32,8,3584]{2,1,0:T(8,128)(2,1)}, f32[2,128]{1,0:T(2,128)}, f32[32,8,3584]{2,1,0:T(8,128)S(1)}, f32[32,8...) custom-call(s32[1]{0:T(128)} %bitcast.refs_0_.refs_9_, ...), custom_call_target="tpu_custom_call", output_to_operand_aliasing={{3}: (8, {}), {4}: (9, {}), {5}: (10, {})} | custom-call | flops 10000000 | bytes 10000000 | tf_op jit(solution)/shard_map/combine/pallas_call | solution.py:431
  (98 shorter events, 34.3 us)
Async XLA Ops:
  1.9 14.0 %collective-permute-start = (bf16[128,3584]{1,0:T(8,128)(2,1)S(1)}, bf16[128,3584]{1,0:T(8,128)(2,1)S(1)}, u32[]{:S(2)}, u32[]{:S(2)}) collective-permute-start(bf16[128,3584]{1,0:T(8,128)(2,1)S(1)} %slice.3), channel_id=1, source_target_pairs={{0,1},{1,2},{2,3},{3,4},{4,5},{5,6},{6,7},{7,8},{8,9},{9,10},{10,1... | collective-permute-start | bytes 2752520 | tf_op jit(solution)/shard_map/ppermute | solution.py:318
  9.6 39.4 %copy-start.19 = (bf16[2048,896]{1,0:T(8,128)(2,1)S(1)}, bf16[2048,896]{1,0:T(8,128)(2,1)}, u32[]{:S(2)}) copy-start(bf16[2048,896]{1,0:T(8,128)(2,1)} %refs_5_.7) | copy-start | bytes 11010052
  20.8 10.6 %collective-permute-start.1 = (bf16[7,8,8,128]{3,2,1,0:T(8,128)(2,1)S(1)}, bf16[7,8,8,128]{3,2,1,0:T(8,128)(2,1)S(1)}, u32[]{:S(2)}, u32[]{:S(2)}) collective-permute-start(bf16[7,8,8,128]{3,2,1,0:T(8,128)(2,1)S(1)} %get-tuple-element.42), channel_id=1, source_target_pairs={{0,12},{1,13},{2,14},{3,15},{4,8},{5,9},{6,10},{7,11},{8,4},{9,5},... | collective-permute-start | bytes 344072 | tf_op jit(solution)/shard_map/ppermute | solution.py:370
  21.4 12.0 %collective-permute-start.2 = (bf16[7,8,8,128]{3,2,1,0:T(8,128)(2,1)S(1)}, bf16[7,8,8,128]{3,2,1,0:T(8,128)(2,1)S(1)}, u32[]{:S(2)}, u32[]{:S(2)}) collective-permute-start(bf16[7,8,8,128]{3,2,1,0:T(8,128)(2,1)S(1)} %get-tuple-element.43), channel_id=1, source_target_pairs={{0,13},{1,12},{2,15},{3,14},{4,9},{5,8},{6,11},{7,10},{8,5},{9,4},... | collective-permute-start | bytes 344072 | tf_op jit(solution)/shard_map/ppermute | solution.py:370
  26.4 8.7 %collective-permute-start.12 = (bf16[7,8,8,128]{3,2,1,0:T(8,128)(2,1)S(1)}, bf16[7,8,8,128]{3,2,1,0:T(8,128)(2,1)S(1)}, u32[]{:S(2)}, u32[]{:S(2)}) collective-permute-start(bf16[7,8,8,128]{3,2,1,0:T(8,128)(2,1)S(1)} %get-tuple-element.55), channel_id=1, source_target_pairs={{0,4},{1,5},{2,6},{3,7},{4,0},{5,1},{6,2},{7,3},{8,12},{9,13},{10,... | collective-permute-start | bytes 344072 | tf_op jit(solution)/shard_map/ppermute | solution.py:370
  29.1 7.3 %collective-permute-start.13 = (bf16[7,8,8,128]{3,2,1,0:T(8,128)(2,1)S(1)}, bf16[7,8,8,128]{3,2,1,0:T(8,128)(2,1)S(1)}, u32[]{:S(2)}, u32[]{:S(2)}) collective-permute-start(bf16[7,8,8,128]{3,2,1,0:T(8,128)(2,1)S(1)} %get-tuple-element.56), channel_id=1, source_target_pairs={{0,5},{1,4},{2,7},{3,6},{4,1},{5,0},{6,3},{7,2},{8,13},{9,12},{10,... | collective-permute-start | bytes 344072 | tf_op jit(solution)/shard_map/ppermute | solution.py:370
  29.2 9.6 %collective-permute-start.14 = (bf16[7,8,8,128]{3,2,1,0:T(8,128)(2,1)S(1)}, bf16[7,8,8,128]{3,2,1,0:T(8,128)(2,1)S(1)}, u32[]{:S(2)}, u32[]{:S(2)}) collective-permute-start(bf16[7,8,8,128]{3,2,1,0:T(8,128)(2,1)S(1)} %get-tuple-element.57), channel_id=1, source_target_pairs={{0,6},{1,7},{2,4},{3,5},{4,2},{5,3},{6,0},{7,1},{8,14},{9,15},{10,... | collective-permute-start | bytes 344072 | tf_op jit(solution)/shard_map/ppermute | solution.py:370
  31.4 11.9 %collective-permute-start.15 = (bf16[7,8,8,128]{3,2,1,0:T(8,128)(2,1)S(1)}, bf16[7,8,8,128]{3,2,1,0:T(8,128)(2,1)S(1)}, u32[]{:S(2)}, u32[]{:S(2)}) collective-permute-start(bf16[7,8,8,128]{3,2,1,0:T(8,128)(2,1)S(1)} %get-tuple-element.58), channel_id=1, source_target_pairs={{0,7},{1,6},{2,5},{3,4},{4,3},{5,2},{6,1},{7,0},{8,15},{9,14},{10,... | collective-permute-start | bytes 344072 | tf_op jit(solution)/shard_map/ppermute | solution.py:370
  33.4 21.3 %collective-permute-start.3 = (bf16[7,8,8,128]{3,2,1,0:T(8,128)(2,1)S(1)}, bf16[7,8,8,128]{3,2,1,0:T(8,128)(2,1)S(1)}, u32[]{:S(2)}, u32[]{:S(2)}) collective-permute-start(bf16[7,8,8,128]{3,2,1,0:T(8,128)(2,1)S(1)} %get-tuple-element.44), channel_id=1, source_target_pairs={{0,14},{1,15},{2,12},{3,13},{4,10},{5,11},{6,8},{7,9},{8,6},{9,7},... | collective-permute-start | bytes 344072 | tf_op jit(solution)/shard_map/ppermute | solution.py:370
  35.1 19.6 %collective-permute-start.8 = (bf16[7,8,8,128]{3,2,1,0:T(8,128)(2,1)S(1)}, bf16[7,8,8,128]{3,2,1,0:T(8,128)(2,1)S(1)}, u32[]{:S(2)}, u32[]{:S(2)}) collective-permute-start(bf16[7,8,8,128]{3,2,1,0:T(8,128)(2,1)S(1)} %get-tuple-element.51), channel_id=1, source_target_pairs={{0,8},{1,9},{2,10},{3,11},{4,12},{5,13},{6,14},{7,15},{8,0},{9,1},... | collective-permute-start | bytes 344072 | tf_op jit(solution)/shard_map/ppermute | solution.py:370
  36.5 19.9 %collective-permute-start.9 = (bf16[7,8,8,128]{3,2,1,0:T(8,128)(2,1)S(1)}, bf16[7,8,8,128]{3,2,1,0:T(8,128)(2,1)S(1)}, u32[]{:S(2)}, u32[]{:S(2)}) collective-permute-start(bf16[7,8,8,128]{3,2,1,0:T(8,128)(2,1)S(1)} %get-tuple-element.52), channel_id=1, source_target_pairs={{0,9},{1,8},{2,11},{3,10},{4,13},{5,12},{6,15},{7,14},{8,1},{9,0},... | collective-permute-start | bytes 344072 | tf_op jit(solution)/shard_map/ppermute | solution.py:370
  38.8 22.5 %collective-permute-start.10 = (bf16[7,8,8,128]{3,2,1,0:T(8,128)(2,1)S(1)}, bf16[7,8,8,128]{3,2,1,0:T(8,128)(2,1)S(1)}, u32[]{:S(2)}, u32[]{:S(2)}) collective-permute-start(bf16[7,8,8,128]{3,2,1,0:T(8,128)(2,1)S(1)} %get-tuple-element.53), channel_id=1, source_target_pairs={{0,10},{1,11},{2,8},{3,9},{4,14},{5,15},{6,12},{7,13},{8,2},{9,3},... | collective-permute-start | bytes 344072 | tf_op jit(solution)/shard_map/ppermute | solution.py:370
  43.3 20.4 %collective-permute-start.11 = (bf16[7,8,8,128]{3,2,1,0:T(8,128)(2,1)S(1)}, bf16[7,8,8,128]{3,2,1,0:T(8,128)(2,1)S(1)}, u32[]{:S(2)}, u32[]{:S(2)}) collective-permute-start(bf16[7,8,8,128]{3,2,1,0:T(8,128)(2,1)S(1)} %get-tuple-element.54), channel_id=1, source_target_pairs={{0,11},{1,10},{2,9},{3,8},{4,15},{5,14},{6,13},{7,12},{8,3},{9,2},... | collective-permute-start | bytes 344072 | tf_op jit(solution)/shard_map/ppermute | solution.py:370
  54.6 18.0 %collective-permute-start.4 = (bf16[7,8,8,128]{3,2,1,0:T(8,128)(2,1)S(1)}, bf16[7,8,8,128]{3,2,1,0:T(8,128)(2,1)S(1)}, u32[]{:S(2)}, u32[]{:S(2)}) collective-permute-start(bf16[7,8,8,128]{3,2,1,0:T(8,128)(2,1)S(1)} %get-tuple-element.45), channel_id=1, source_target_pairs={{0,15},{1,14},{2,13},{3,12},{4,11},{5,10},{6,9},{7,8},{8,7},{9,6},... | collective-permute-start | bytes 344072 | tf_op jit(solution)/shard_map/ppermute | solution.py:370
  54.7 18.0 %collective-permute-start.5 = (bf16[7,8,8,128]{3,2,1,0:T(8,128)(2,1)S(1)}, bf16[7,8,8,128]{3,2,1,0:T(8,128)(2,1)S(1)}, u32[]{:S(2)}, u32[]{:S(2)}) collective-permute-start(bf16[7,8,8,128]{3,2,1,0:T(8,128)(2,1)S(1)} %get-tuple-element.48), channel_id=1, source_target_pairs={{0,1},{1,0},{2,3},{3,2},{4,5},{5,4},{6,7},{7,6},{8,9},{9,8},{10,11... | collective-permute-start | bytes 344072 | tf_op jit(solution)/shard_map/ppermute | solution.py:370
  56.3 18.0 %collective-permute-start.6 = (bf16[7,8,8,128]{3,2,1,0:T(8,128)(2,1)S(1)}, bf16[7,8,8,128]{3,2,1,0:T(8,128)(2,1)S(1)}, u32[]{:S(2)}, u32[]{:S(2)}) collective-permute-start(bf16[7,8,8,128]{3,2,1,0:T(8,128)(2,1)S(1)} %get-tuple-element.49), channel_id=1, source_target_pairs={{0,2},{1,3},{2,0},{3,1},{4,6},{5,7},{6,4},{7,5},{8,10},{9,11},{10,... | collective-permute-start | bytes 344072 | tf_op jit(solution)/shard_map/ppermute | solution.py:370
  61.3 14.4 %collective-permute-start.7 = (bf16[7,8,8,128]{3,2,1,0:T(8,128)(2,1)S(1)}, bf16[7,8,8,128]{3,2,1,0:T(8,128)(2,1)S(1)}, u32[]{:S(2)}, u32[]{:S(2)}) collective-permute-start(bf16[7,8,8,128]{3,2,1,0:T(8,128)(2,1)S(1)} %get-tuple-element.50), channel_id=1, source_target_pairs={{0,3},{1,2},{2,1},{3,0},{4,7},{5,6},{6,5},{7,4},{8,11},{9,10},{10,... | collective-permute-start | bytes 344072 | tf_op jit(solution)/shard_map/ppermute | solution.py:370
  63.7 13.8 %collective-permute-start.24 = (bf16[113,8,128]{2,1,0:T(8,128)(2,1)S(1)}, bf16[113,8,128]{2,1,0:T(8,128)(2,1)S(1)}, u32[]{:S(2)}, u32[]{:S(2)}) collective-permute-start(bf16[113,8,128]{2,1,0:T(8,128)(2,1)S(1)} %get-tuple-element.69), channel_id=1, source_target_pairs={{0,5},{1,4},{2,7},{3,6},{4,1},{5,0},{6,3},{7,2},{8,13},{9,12},{10,... | collective-permute-start | bytes 694280 | tf_op jit(solution)/shard_map/ppermute | solution.py:370
  72.6 29.0 %collective-permute-start.23 = (bf16[113,8,128]{2,1,0:T(8,128)(2,1)S(1)}, bf16[113,8,128]{2,1,0:T(8,128)(2,1)S(1)}, u32[]{:S(2)}, u32[]{:S(2)}) collective-permute-start(bf16[113,8,128]{2,1,0:T(8,128)(2,1)S(1)} %get-tuple-element.59.refs_9_), channel_id=1, source_target_pairs={{0,4},{1,5},{2,6},{3,7},{4,0},{5,1},{6,2},{7,3},{8,12},{9,13},{10,... | collective-permute-start | bytes 694280 | tf_op jit(solution)/shard_map/ppermute | solution.py:370
  72.7 19.7 %collective-permute-start.25 = (bf16[113,8,128]{2,1,0:T(8,128)(2,1)S(1)}, bf16[113,8,128]{2,1,0:T(8,128)(2,1)S(1)}, u32[]{:S(2)}, u32[]{:S(2)}) collective-permute-start(bf16[113,8,128]{2,1,0:T(8,128)(2,1)S(1)} %get-tuple-element.70), channel_id=1, source_target_pairs={{0,6},{1,7},{2,4},{3,5},{4,2},{5,3},{6,0},{7,1},{8,14},{9,15},{10,... | collective-permute-start | bytes 694280 | tf_op jit(solution)/shard_map/ppermute | solution.py:370
  74.3 23.0 %collective-permute-start.26 = (bf16[113,8,128]{2,1,0:T(8,128)(2,1)S(1)}, bf16[113,8,128]{2,1,0:T(8,128)(2,1)S(1)}, u32[]{:S(2)}, u32[]{:S(2)}) collective-permute-start(bf16[113,8,128]{2,1,0:T(8,128)(2,1)S(1)} %get-tuple-element.71), channel_id=1, source_target_pairs={{0,7},{1,6},{2,5},{3,4},{4,3},{5,2},{6,1},{7,0},{8,15},{9,14},{10,... | collective-permute-start | bytes 694280 | tf_op jit(solution)/shard_map/ppermute | solution.py:370
  75.6 26.3 %collective-permute-start.28 = (bf16[113,8,128]{2,1,0:T(8,128)(2,1)S(1)}, bf16[113,8,128]{2,1,0:T(8,128)(2,1)S(1)}, u32[]{:S(2)}, u32[]{:S(2)}) collective-permute-start(bf16[113,8,128]{2,1,0:T(8,128)(2,1)S(1)} %get-tuple-element.72), channel_id=1, source_target_pairs={{0,9},{1,8},{2,11},{3,10},{4,13},{5,12},{6,15},{7,14},{8,1},{9,0},... | collective-permute-start | bytes 694280 | tf_op jit(solution)/shard_map/ppermute | solution.py:370
  77.5 25.3 %collective-permute-start.29 = (bf16[113,8,128]{2,1,0:T(8,128)(2,1)S(1)}, bf16[113,8,128]{2,1,0:T(8,128)(2,1)S(1)}, u32[]{:S(2)}, u32[]{:S(2)}) collective-permute-start(bf16[113,8,128]{2,1,0:T(8,128)(2,1)S(1)} %get-tuple-element.73), channel_id=1, source_target_pairs={{0,10},{1,11},{2,8},{3,9},{4,14},{5,15},{6,12},{7,13},{8,2},{9,3},... | collective-permute-start | bytes 694280 | tf_op jit(solution)/shard_map/ppermute | solution.py:370
  92.5 28.1 %collective-permute-start.27 = (bf16[113,8,128]{2,1,0:T(8,128)(2,1)S(1)}, bf16[113,8,128]{2,1,0:T(8,128)(2,1)S(1)}, u32[]{:S(2)}, u32[]{:S(2)}) collective-permute-start(bf16[113,8,128]{2,1,0:T(8,128)(2,1)S(1)} %get-tuple-element.60.refs_9_), channel_id=1, source_target_pairs={{0,8},{1,9},{2,10},{3,11},{4,12},{5,13},{6,14},{7,15},{8,0},{9,1},... | collective-permute-start | bytes 694280 | tf_op jit(solution)/shard_map/ppermute | solution.py:370
  97.4 21.5 %collective-permute-start.30 = (bf16[113,8,128]{2,1,0:T(8,128)(2,1)S(1)}, bf16[113,8,128]{2,1,0:T(8,128)(2,1)S(1)}, u32[]{:S(2)}, u32[]{:S(2)}) collective-permute-start(bf16[113,8,128]{2,1,0:T(8,128)(2,1)S(1)} %get-tuple-element.74), channel_id=1, source_target_pairs={{0,11},{1,10},{2,9},{3,8},{4,15},{5,14},{6,13},{7,12},{8,3},{9,2},... | collective-permute-start | bytes 694280 | tf_op jit(solution)/shard_map/ppermute | solution.py:370
  101.6 20.9 %collective-permute-start.20 = (bf16[113,8,128]{2,1,0:T(8,128)(2,1)S(1)}, bf16[113,8,128]{2,1,0:T(8,128)(2,1)S(1)}, u32[]{:S(2)}, u32[]{:S(2)}) collective-permute-start(bf16[113,8,128]{2,1,0:T(8,128)(2,1)S(1)} %get-tuple-element.66), channel_id=1, source_target_pairs={{0,1},{1,0},{2,3},{3,2},{4,5},{5,4},{6,7},{7,6},{8,9},{9,8},{10,11... | collective-permute-start | bytes 694280 | tf_op jit(solution)/shard_map/ppermute | solution.py:370
  102.0 22.6 %collective-permute-start.21 = (bf16[113,8,128]{2,1,0:T(8,128)(2,1)S(1)}, bf16[113,8,128]{2,1,0:T(8,128)(2,1)S(1)}, u32[]{:S(2)}, u32[]{:S(2)}) collective-permute-start(bf16[113,8,128]{2,1,0:T(8,128)(2,1)S(1)} %get-tuple-element.67), channel_id=1, source_target_pairs={{0,2},{1,3},{2,0},{3,1},{4,6},{5,7},{6,4},{7,5},{8,10},{9,11},{10,... | collective-permute-start | bytes 694280 | tf_op jit(solution)/shard_map/ppermute | solution.py:370
  102.8 23.5 %collective-permute-start.22 = (bf16[113,8,128]{2,1,0:T(8,128)(2,1)}, bf16[113,8,128]{2,1,0:T(8,128)(2,1)}, u32[]{:S(2)}, u32[]{:S(2)}) collective-permute-start(bf16[113,8,128]{2,1,0:T(8,128)(2,1)} %get-tuple-element.68), channel_id=1, source_target_pairs={{0,3},{1,2},{2,1},{3,0},{4,7},{5,6},{6,5},{7,4},{8,11},{9,10},{10,... | collective-permute-start | bytes 694280 | tf_op jit(solution)/shard_map/ppermute | solution.py:370
  119.6 25.5 %collective-permute-start.16 = (bf16[113,8,128]{2,1,0:T(8,128)(2,1)}, bf16[113,8,128]{2,1,0:T(8,128)(2,1)S(1)}, u32[]{:S(2)}, u32[]{:S(2)}) collective-permute-start(bf16[113,8,128]{2,1,0:T(8,128)(2,1)} %get-tuple-element.62), channel_id=1, source_target_pairs={{0,12},{1,13},{2,14},{3,15},{4,8},{5,9},{6,10},{7,11},{8,4},{9,5},... | collective-permute-start | bytes 694280 | tf_op jit(solution)/shard_map/ppermute | solution.py:370
  121.3 31.7 %collective-permute-start.17 = (bf16[113,8,128]{2,1,0:T(8,128)(2,1)}, bf16[113,8,128]{2,1,0:T(8,128)(2,1)S(1)}, u32[]{:S(2)}, u32[]{:S(2)}) collective-permute-start(bf16[113,8,128]{2,1,0:T(8,128)(2,1)} %get-tuple-element.63), channel_id=1, source_target_pairs={{0,13},{1,12},{2,15},{3,14},{4,9},{5,8},{6,11},{7,10},{8,5},{9,4},... | collective-permute-start | bytes 694280 | tf_op jit(solution)/shard_map/ppermute | solution.py:370
  123.1 33.3 %collective-permute-start.18 = (bf16[113,8,128]{2,1,0:T(8,128)(2,1)}, bf16[113,8,128]{2,1,0:T(8,128)(2,1)S(1)}, u32[]{:S(2)}, u32[]{:S(2)}) collective-permute-start(bf16[113,8,128]{2,1,0:T(8,128)(2,1)} %get-tuple-element.64), channel_id=1, source_target_pairs={{0,14},{1,15},{2,12},{3,13},{4,10},{5,11},{6,8},{7,9},{8,6},{9,7},... | collective-permute-start | bytes 694280 | tf_op jit(solution)/shard_map/ppermute | solution.py:370
  125.3 36.8 %collective-permute-start.19 = (bf16[113,8,128]{2,1,0:T(8,128)(2,1)}, bf16[113,8,128]{2,1,0:T(8,128)(2,1)S(1)}, u32[]{:S(2)}, u32[]{:S(2)}) collective-permute-start(bf16[113,8,128]{2,1,0:T(8,128)(2,1)} %get-tuple-element.65), channel_id=1, source_target_pairs={{0,15},{1,14},{2,13},{3,12},{4,11},{5,10},{6,9},{7,8},{8,7},{9,6},... | collective-permute-start | bytes 694280 | tf_op jit(solution)/shard_map/ppermute | solution.py:370
  (24 other events, 273.9 us)
where the time goes:
time: 169 us; the launch traced here: 167 us
  starting transfers between devices  53.2 us (31%)
  waiting for transfers between devices  50.7 us (30%)
  Pallas kernels  46.9 us (28%)
  local copies, waits for them, and re-layouts  15.7 us (9%)
    ppermute x30, starting transfers between devices, exchange(): return lax.ppermute(block, 'seq', [(i, i ^ pattern) for i in range(groups)])  49.5 us
    ppermute x30, waiting for transfers between devices, exchange(): return lax.ppermute(block, 'seq', [(i, i ^ pattern) for i in range(groups)])  46.9 us
    pallas_call x4, Pallas kernels, program(): features_call(*[arrived[s].reshape(KEEP, rows, BLK) for s in members], en...  24.2 us
    unnamed x53, local copies, waits for them, and re-layouts  13.5 us
    pallas_call x2, Pallas kernels, combine(): pl.pallas_call(functools.partial(combine_kernel, groups, cap, fanout, seg...  12 us
    pallas_call x1, Pallas kernels, program(): pl.pallas_call(functools.partial(far_kernel, groups, fanout, windows), ou...  4.84 us
    ppermute x1, waiting for transfers between devices, program(): lax.ppermute(corpus[-LEN:], 'seq', [(i, i + 1) for i in range(groups - 1)])  3.8 us
    ppermute x1, starting transfers between devices, program(): lax.ppermute(corpus[-LEN:], 'seq', [(i, i + 1) for i in range(groups - 1)])  3.71 us
  transfers between devices with their start and end apart: 31, of which 14 were waited for; matrix products, arithmetic and copies ran while one was open for 2% of the time, Pallas kernels for 22%

commit v1 on v0

--- a/solution.py
+++ b/solution.py
@@ -22,9 +22,14 @@
 ANY = pl.BlockSpec(memory_space=pl.ANY)
 
 
+def quarters(groups):
+    quarter = groups // 4
+    return [list(range(part * quarter, (part + 1) * quarter)) for part in range(4)]
+
+
 def send_order(groups):
-    quarter = groups // 4
-    return [s for part in (2, 1, 3, 0) for s in range(part * quarter, (part + 1) * quarter)]
+    own, near, far, last = quarters(groups)
+    return far[:1] + near + far[1:] + last + own[1:]
 
 
 def clear_counts(counts, groups):
@@ -53,18 +58,15 @@
     lax.fori_loop(0, rows // 16, body, 0)
 
 
-def place_items(t, fanout, lowest, members, me, routes_ref, in_ref, counts, normal_ref, stage):
+def place_items(t, fanout, me, routes_ref, in_ref, counts, normal_ref, stage):
     for k in range(fanout):
         group = routes_ref[t * fanout + k]
         slot = counts[group]
         counts[group] = slot + 1
-        partner = (group ^ me) - lowest
-
-        @pl.when(jnp.logical_and(partner >= 0, partner < members))
-        def _():
-            for q in range(KEEP):
-                at = pl.multiple_of(in_ref[group * KEEP + q] * BLK, BLK)
-                stage[partner, q, slot] = normal_ref[t, :, pl.ds(at, BLK)]
+        partner = group ^ me
+        for q in range(KEEP):
+            at = pl.multiple_of(in_ref[group * KEEP + q] * BLK, BLK)
+            stage[partner, q, slot] = normal_ref[t, :, pl.ds(at, BLK)]
 
 
 def send_stage(stage, outs, sems):
@@ -77,12 +79,11 @@
         copy.wait()
 
 
-def far_kernel(groups, fanout, windows, *refs):
-    members = groups // 2
+def pack_kernel(groups, fanout, windows, *refs):
     me_ref, ends_ref, routes_ref, in_ref, gain_ref, own_ref, below_ref = refs[:7]
     normal_ref = refs[7]
-    outs = refs[8 : 8 + members]
-    ext, stage, counts, sems = refs[8 + members :]
+    outs = refs[8 : 8 + groups]
+    ext, stage, counts, sems = refs[8 + groups :]
     width = own_ref.shape[1]
     gain = gain_ref[...]
 
@@ -115,10 +116,7 @@
                 pltpu.roll(high_rows, turn, 0),
             )
             normal_ref[t] = rows.astype(jnp.bfloat16)
-            place_items(
-                t, fanout, groups - members, members, me, routes_ref, in_ref, counts,
-                normal_ref, stage,
-            )
+            place_items(t, fanout, me, routes_ref, in_ref, counts, normal_ref, stage)
 
         def from_below(j, carry):
             low = pl.multiple_of(base + j * SEG, SEG)
@@ -134,24 +132,6 @@
         split = jnp.clip((LEN - base) // SEG, 0, segs_per_window)
         lax.fori_loop(0, split, from_below, 0)
         lax.fori_loop(split, segs_per_window, from_own, 0)
-    send_stage(stage, outs, sems)
-
-
-def near_kernel(groups, fanout, *refs):
-    members = groups // 2
-    me_ref, routes_ref, in_ref, normal_ref = refs[:4]
-    outs = refs[4 : 4 + members]
-    stage, counts, sems = refs[4 + members :]
-    clear_counts(counts, groups)
-    me = me_ref[0]
-
-    def body(t, carry):
-        place_items(
-            t, fanout, 0, members, me, routes_ref, in_ref, counts, normal_ref, stage
-        )
-        return carry
-
-    lax.fori_loop(0, normal_ref.shape[0], body, 0)
     send_stage(stage, outs, sems)
 
 
@@ -331,38 +311,23 @@
         compiler_params=pltpu.CompilerParams(vmem_limit_bytes=12 << 20),
         name="own",
     )(norm_gain.reshape(1, -1), corpus)
-    half = groups // 2
-    slots = jax.ShapeDtypeStruct((KEEP, cap, SEG, BLK), jnp.bfloat16)
-    pack_scratch = [
-        pltpu.VMEM((half, KEEP, cap, SEG, BLK), jnp.bfloat16),
-        pltpu.SMEM((groups,), jnp.int32),
-        pltpu.SemaphoreType.DMA((half,)),
-    ]
-    far = pl.pallas_call(
-        functools.partial(far_kernel, groups, fanout, windows),
+    packed = pl.pallas_call(
+        functools.partial(pack_kernel, groups, fanout, windows),
         out_shape=(jax.ShapeDtypeStruct((segments, SEG, width), jnp.bfloat16),)
-        + (slots,) * half,
+        + (jax.ShapeDtypeStruct((KEEP, cap, SEG, BLK), jnp.bfloat16),) * groups,
         in_specs=[SMEM] * 4 + [VMEM] * 3,
-        out_specs=(VMEM,) + (ANY,) * half,
-        scratch_shapes=[pltpu.VMEM((LEN + SEG, width), jnp.float32)] + pack_scratch,
+        out_specs=(VMEM,) + (ANY,) * groups,
+        scratch_shapes=[
+            pltpu.VMEM((LEN + SEG, width), jnp.float32),
+            pltpu.VMEM((groups, KEEP, cap, SEG, BLK), jnp.bfloat16),
+            pltpu.SMEM((groups,), jnp.int32),
+            pltpu.SemaphoreType.DMA((groups,)),
+        ],
         cost_estimate=pl.CostEstimate(flops=10_000_000, bytes_accessed=8_000_000, transcendentals=0),
         compiler_params=pltpu.CompilerParams(vmem_limit_bytes=16 << 20),
-        name="far",
+        name="pack",
     )(me, window_ends, flat_routes, flat_in, norm_gain.reshape(1, -1), own, below)
-    normal = far[0]
-    near = pl.pallas_call(
-        functools.partial(near_kernel, groups, fanout),
-        out_shape=(slots,) * half,
-        in_specs=[SMEM] * 3 + [VMEM],
-        out_specs=(ANY,) * half,
-        scratch_shapes=pack_scratch,
-        cost_estimate=pl.CostEstimate(
-            flops=10_000_000, bytes_accessed=4_000_000, transcendentals=0
-        ),
-        compiler_params=pltpu.CompilerParams(vmem_limit_bytes=8 << 20),
-        name="near",
-    )(me, flat_routes, flat_in, normal)
-    outgoing = tuple(near) + tuple(far[1:])
+    normal, outgoing = packed[0], packed[1:]
 
     def exchange(block, pattern):
         if pattern == 0:
@@ -370,7 +335,7 @@
         return lax.ppermute(block, "seq", [(i, i ^ pattern) for i in range(groups)])
 
     quarter = groups // 4
-    arrived = {}
+    arrived = {0: outgoing[0]}
     for s in send_order(groups):
         arrived[s] = exchange(outgoing[s], s)
 

time: 169 us -> 170 us (level)
  waiting for transfers between devices: 50.7 us -> 64 us
  starting transfers between devices: 53.2 us -> 42.9 us
  Pallas kernels: 46.9 us -> 44.9 us
    ppermute x30, waiting for transfers between devices: 46.9 us -> 60.2 us  [exchange(): return lax.ppermute(block, 'seq', [(i, i ^ pattern) for i in range(groups)])]
    ppermute x30, starting transfers between devices: 49.5 us -> 39.2 us  [exchange(): return lax.ppermute(block, 'seq', [(i, i ^ pattern) for i in range(groups)])]
    pallas_call x2 -> x1, Pallas kernels: 8.12 us -> 6.14 us  [program(): pl.pallas_call(functools.partial(pack_kernel, groups, fanout, windows), o...]
  transfers between devices with their start and end apart: 31 -> 31, of which waited for: 14 -> 16; matrix products, arithmetic and copies ran while one was open for 2% -> 2% of each run, Pallas kernels for 22% -> 20%
where the time goes in v1:
time: 170 us; the launch traced here: 168 us
  waiting for transfers between devices  64 us (38%)
  Pallas kernels  44.9 us (26%)
  starting transfers between devices  42.9 us (25%)
  local copies, waits for them, and re-layouts  15.7 us (9%)
    ppermute x30, waiting for transfers between devices, exchange(): return lax.ppermute(block, 'seq', [(i, i ^ pattern) for i in range(groups)])  60.2 us
    ppermute x30, starting transfers between devices, exchange(): return lax.ppermute(block, 'seq', [(i, i ^ pattern) for i in range(groups)])  39.2 us
    pallas_call x4, Pallas kernels, program(): features_call(*[arrived[s].reshape(KEEP, rows, BLK) for s in members], en...  24.2 us
    unnamed x53, local copies, waits for them, and re-layouts  13.5 us
    pallas_call x2, Pallas kernels, combine(): pl.pallas_call(functools.partial(combine_kernel, groups, cap, fanout, seg...  12 us
    pallas_call x1, Pallas kernels, program(): pl.pallas_call(functools.partial(pack_kernel, groups, fanout, windows), o...  6.14 us
    ppermute x1, waiting for transfers between devices, program(): lax.ppermute(corpus[-LEN:], 'seq', [(i, i + 1) for i in range(groups - 1)])  3.8 us
    ppermute x1, starting transfers between devices, program(): lax.ppermute(corpus[-LEN:], 'seq', [(i, i + 1) for i in range(groups - 1)])  3.71 us
  transfers between devices with their start and end apart: 31, of which 16 were waited for; matrix products, arithmetic and copies ran while one was open for 2% of the time, Pallas kernels for 20%

profile of v1, /device:TPU:13, one launch (start us, length us, event | category | flops | bytes accessed | tf_op | source)
XLA Modules:
  0.0 168.4 jit_solution(15787322800536892276)
XLA Ops:
  1.9 3.7 %collective-permute-start = (bf16[128,3584]{1,0:T(8,128)(2,1)S(1)}, bf16[128,3584]{1,0:T(8,128)(2,1)S(1)}, u32[]{:S(2)}, u32[]{:S(2)}) collective-permute-start(bf16[128,3584]{1,0:T(8,128)(2,1)S(1)} %slice.3), channel_id=1, source_target_pairs={{0,1},{1,2},{2,3},{3,4},{4,5},{5,6},{6,7},{7,8},{8,9},{9,10},{10,1... | collective-permute-start | bytes 2752520 | tf_op jit(solution)/shard_map/ppermute | solution.py:298
  9.6 2.5 %own.1.refs_5_ = f32[256,3584]{1,0:T(8,128)S(1)} custom-call(f32[1,3584]{1,0:T(1,128)S(1)} %reshape.104.gain_ref.refs_4_, bf16[256,3584]{1,0:T(8,128)(2,1)S(1)} %copy-done), custom_call_target="tpu_custom_call" | custom-call | flops 5505024 | bytes 5505024 | tf_op jit(solution)/shard_map/own/pallas_call | solution.py:303
  12.1 3.8 %collective-permute-done.refs_6_ = bf16[128,3584]{1,0:T(8,128)(2,1)S(1)} collective-permute-done((bf16[128,3584]{1,0:T(8,128)(2,1)S(1)}, bf16[128,3584]{1,0:T(8,128)(2,1)S(1)}, u32[]{:S(2)}, u32[]{:S(2)}) %collective-permute-start) | collective-permute-done | bytes 917536 | tf_op jit(solution)/shard_map/ppermute | solution.py:298
  15.9 6.1 %pack.1 = (bf16[32,8,3584]{2,1,0:T(8,128)(2,1)S(1)}, bf16[7,8,8,128]{3,2,1,0:T(8,128)(2,1)S(1)}, bf16[7,8,8,128]{3,2,1,0:T(8,128)(2,1)S(1)}, bf16[7,8,8,128]{3,2...) custom-call(s32[1]{0:T(128)} %bitcast.refs_0_.refs_9_, ...), custom_call_target="tpu_custom_call" | custom-call | flops 10000000 | bytes 8000000 | tf_op jit(solution)/shard_map/pack/pallas_call | solution.py:314
  22.7 1.9 %collective-permute-start.2 = (bf16[7,8,8,128]{3,2,1,0:T(8,128)(2,1)S(1)}, bf16[7,8,8,128]{3,2,1,0:T(8,128)(2,1)S(1)}, u32[]{:S(2)}, u32[]{:S(2)}) collective-permute-start(bf16[7,8,8,128]{3,2,1,0:T(8,128)(2,1)S(1)} %get-tuple-element.43), channel_id=1, source_target_pairs={{0,13},{1,12},{2,15},{3,14},{4,9},{5,8},{6,11},{7,10},{8,5},{9,4},... | collective-permute-start | bytes 344072 | tf_op jit(solution)/shard_map/ppermute | solution.py:335
  24.6 2.5 %collective-permute-start.12 = (bf16[7,8,8,128]{3,2,1,0:T(8,128)(2,1)S(1)}, bf16[7,8,8,128]{3,2,1,0:T(8,128)(2,1)S(1)}, u32[]{:S(2)}, u32[]{:S(2)}) collective-permute-start(bf16[7,8,8,128]{3,2,1,0:T(8,128)(2,1)S(1)} %get-tuple-element.54), channel_id=1, source_target_pairs={{0,4},{1,5},{2,6},{3,7},{4,0},{5,1},{6,2},{7,3},{8,12},{9,13},{10,... | collective-permute-start | bytes 344072 | tf_op jit(solution)/shard_map/ppermute | solution.py:335
  27.2 2.1 %collective-permute-start.14 = (bf16[7,8,8,128]{3,2,1,0:T(8,128)(2,1)S(1)}, bf16[7,8,8,128]{3,2,1,0:T(8,128)(2,1)S(1)}, u32[]{:S(2)}, u32[]{:S(2)}) collective-permute-start(bf16[7,8,8,128]{3,2,1,0:T(8,128)(2,1)S(1)} %get-tuple-element.56), channel_id=1, source_target_pairs={{0,6},{1,7},{2,4},{3,5},{4,2},{5,3},{6,0},{7,1},{8,14},{9,15},{10,... | collective-permute-start | bytes 344072 | tf_op jit(solution)/shard_map/ppermute | solution.py:335
  31.2 3.5 %collective-permute-done.2 = bf16[7,8,8,128]{3,2,1,0:T(8,128)(2,1)S(1)} collective-permute-done((bf16[7,8,8,128]{3,2,1,0:T(8,128)(2,1)S(1)}, bf16[7,8,8,128]{3,2,1,0:T(8,128)(2,1)S(1)}, u32[]{:S(2)}, u32[]{:S(2)}) %collective-permute-start.2) | collective-permute-done | bytes 114720 | tf_op jit(solution)/shard_map/ppermute | solution.py:335
  39.3 2.8 %collective-permute-start.10 = (bf16[7,8,8,128]{3,2,1,0:T(8,128)(2,1)S(1)}, bf16[7,8,8,128]{3,2,1,0:T(8,128)(2,1)S(1)}, u32[]{:S(2)}, u32[]{:S(2)}) collective-permute-start(bf16[7,8,8,128]{3,2,1,0:T(8,128)(2,1)S(1)} %get-tuple-element.52), channel_id=1, source_target_pairs={{0,10},{1,11},{2,8},{3,9},{4,14},{5,15},{6,12},{7,13},{8,2},{9,3},... | collective-permute-start | bytes 344072 | tf_op jit(solution)/shard_map/ppermute | solution.py:335
  42.1 2.6 %collective-permute-done.15 = bf16[7,8,8,128]{3,2,1,0:T(8,128)(2,1)S(1)} collective-permute-done((bf16[7,8,8,128]{3,2,1,0:T(8,128)(2,1)S(1)}, bf16[7,8,8,128]{3,2,1,0:T(8,128)(2,1)S(1)}, u32[]{:S(2)}, u32[]{:S(2)}) %collective-permute-start.15) | collective-permute-done | bytes 114720 | tf_op jit(solution)/shard_map/ppermute | solution.py:335
  44.7 2.7 %collective-permute-start.11 = (bf16[7,8,8,128]{3,2,1,0:T(8,128)(2,1)S(1)}, bf16[7,8,8,128]{3,2,1,0:T(8,128)(2,1)S(1)}, u32[]{:S(2)}, u32[]{:S(2)}) collective-permute-start(bf16[7,8,8,128]{3,2,1,0:T(8,128)(2,1)S(1)} %get-tuple-element.53), channel_id=1, source_target_pairs={{0,11},{1,10},{2,9},{3,8},{4,15},{5,14},{6,13},{7,12},{8,3},{9,2},... | collective-permute-start | bytes 344072 | tf_op jit(solution)/shard_map/ppermute | solution.py:335
  47.5 5.7 %features.4 = (bf16[113,8,128]{2,1,0:T(8,128)(2,1)S(1)}, bf16[113,8,128]{2,1,0:T(8,128)(2,1)S(1)}, bf16[113,8,128]{2,1,0:T(8,128)(2,1)S(1)}, bf16[113,8,128]{2,1,0:T(8,128)(2,1)S(1)}) custom-call(bf16[7,64,128]{2,1,0:T(8,128)(2,1)S(1)} %bitcast.34, bf16[7,64,128]{2,1,0:T(8,128)(2,1)S(1)} %bitcast.35, bf16[7,64,128]{2,1,0:T(8,128)(2,1)S(1)} %bitcast.37, ...), custom_call_target="tpu_custom_call" | custom-call | flops 2818572288 | bytes 7340032 | tf_op jit(solution)/shard_map/features/pallas_call | solution.py:382
  54.7 5.1 %collective-permute-done.9 = bf16[7,8,8,128]{3,2,1,0:T(8,128)(2,1)S(1)} collective-permute-done((bf16[7,8,8,128]{3,2,1,0:T(8,128)(2,1)S(1)}, bf16[7,8,8,128]{3,2,1,0:T(8,128)(2,1)S(1)}, u32[]{:S(2)}, u32[]{:S(2)}) %collective-permute-start.9) | collective-permute-done | bytes 114720 | tf_op jit(solution)/shard_map/ppermute | solution.py:335
  59.8 2.5 %collective-permute-done.10 = bf16[7,8,8,128]{3,2,1,0:T(8,128)(2,1)S(1)} collective-permute-done((bf16[7,8,8,128]{3,2,1,0:T(8,128)(2,1)S(1)}, bf16[7,8,8,128]{3,2,1,0:T(8,128)(2,1)S(1)}, u32[]{:S(2)}, u32[]{:S(2)}) %collective-permute-start.10) | collective-permute-done | bytes 114720 | tf_op jit(solution)/shard_map/ppermute | solution.py:335
  62.3 2.4 %collective-permute-done.11 = bf16[7,8,8,128]{3,2,1,0:T(8,128)(2,1)S(1)} collective-permute-done((bf16[7,8,8,128]{3,2,1,0:T(8,128)(2,1)S(1)}, bf16[7,8,8,128]{3,2,1,0:T(8,128)(2,1)S(1)}, u32[]{:S(2)}, u32[]{:S(2)}) %collective-permute-start.11) | collective-permute-done | bytes 114720 | tf_op jit(solution)/shard_map/ppermute | solution.py:335
  64.7 3.3 %collective-permute-start.24 = (bf16[113,8,128]{2,1,0:T(8,128)(2,1)S(1)}, bf16[113,8,128]{2,1,0:T(8,128)(2,1)S(1)}, u32[]{:S(2)}, u32[]{:S(2)}) collective-permute-start(bf16[113,8,128]{2,1,0:T(8,128)(2,1)S(1)} %get-tuple-element.68), channel_id=1, source_target_pairs={{0,5},{1,4},{2,7},{3,6},{4,1},{5,0},{6,3},{7,2},{8,13},{9,12},{10,... | collective-permute-start | bytes 694280 | tf_op jit(solution)/shard_map/ppermute | solution.py:335
  68.0 5.7 %features.5 = (bf16[113,8,128]{2,1,0:T(8,128)(2,1)S(1)}, bf16[113,8,128]{2,1,0:T(8,128)(2,1)S(1)}, bf16[113,8,128]{2,1,0:T(8,128)(2,1)S(1)}, bf16[113,8,128]{2,1,0:T(8,128)(2,1)S(1)}) custom-call(bf16[7,64,128]{2,1,0:T(8,128)(2,1)S(1)} %bitcast.29, bf16[7,64,128]{2,1,0:T(8,128)(2,1)S(1)} %bitcast.31, bf16[7,64,128]{2,1,0:T(8,128)(2,1)S(1)} %bitcast.33, ...), custom_call_target="tpu_custom_call" | custom-call | flops 2818572288 | bytes 7340032 | tf_op jit(solution)/shard_map/features/pallas_call | solution.py:382
  76.8 2.2 %collective-permute-start.29 = (bf16[113,8,128]{2,1,0:T(8,128)(2,1)S(1)}, bf16[113,8,128]{2,1,0:T(8,128)(2,1)S(1)}, u32[]{:S(2)}, u32[]{:S(2)}) collective-permute-start(bf16[113,8,128]{2,1,0:T(8,128)(2,1)S(1)} %get-tuple-element.72), channel_id=1, source_target_pairs={{0,10},{1,11},{2,8},{3,9},{4,14},{5,15},{6,12},{7,13},{8,2},{9,3},... | collective-permute-start | bytes 694280 | tf_op jit(solution)/shard_map/ppermute | solution.py:335
  79.0 6.3 %features.6 = (bf16[113,8,128]{2,1,0:T(8,128)(2,1)S(1)}, bf16[113,8,128]{2,1,0:T(8,128)(2,1)S(1)}, bf16[113,8,128]{2,1,0:T(8,128)(2,1)S(1)}, bf16[113,8,128]{2,1,0:T(8,128)(2,1)}) custom-call(bf16[7,64,128]{2,1,0:T(8,128)(2,1)S(1)} %bitcast.26, bf16[7,64,128]{2,1,0:T(8,128)(2,1)S(1)} %bitcast.28, bf16[7,64,128]{2,1,0:T(8,128)(2,1)S(1)} %bitcast.30, ...), custom_call_target="tpu_custom_call" | custom-call | flops 2818572288 | bytes 7340032 | tf_op jit(solution)/shard_map/features/pallas_call | solution.py:382
  85.3 8.2 %collective-permute-done.25.refs_10_ = bf16[113,8,128]{2,1,0:T(8,128)(2,1)S(1)} collective-permute-done((bf16[113,8,128]{2,1,0:T(8,128)(2,1)S(1)}, bf16[113,8,128]{2,1,0:T(8,128)(2,1)S(1)}, u32[]{:S(2)}, u32[]{:S(2)}) %collective-permute-start.25) | collective-permute-done | bytes 231456 | tf_op jit(solution)/shard_map/ppermute | solution.py:335
  93.5 3.2 %collective-permute-start.27 = (bf16[113,8,128]{2,1,0:T(8,128)(2,1)S(1)}, bf16[113,8,128]{2,1,0:T(8,128)(2,1)S(1)}, u32[]{:S(2)}, u32[]{:S(2)}) collective-permute-start(bf16[113,8,128]{2,1,0:T(8,128)(2,1)S(1)} %get-tuple-element.59.refs_9_), channel_id=1, source_target_pairs={{0,8},{1,9},{2,10},{3,11},{4,12},{5,13},{6,14},{7,15},{8,0},{9,1},... | collective-permute-start | bytes 694280 | tf_op jit(solution)/shard_map/ppermute | solution.py:335
  98.5 2.4 %collective-permute-start.30 = (bf16[113,8,128]{2,1,0:T(8,128)(2,1)S(1)}, bf16[113,8,128]{2,1,0:T(8,128)(2,1)S(1)}, u32[]{:S(2)}, u32[]{:S(2)}) collective-permute-start(bf16[113,8,128]{2,1,0:T(8,128)(2,1)S(1)} %get-tuple-element.73), channel_id=1, source_target_pairs={{0,11},{1,10},{2,9},{3,8},{4,15},{5,14},{6,13},{7,12},{8,3},{9,2},... | collective-permute-start | bytes 694280 | tf_op jit(solution)/shard_map/ppermute | solution.py:335
  101.3 2.3 %collective-permute-start.21 = (bf16[113,8,128]{2,1,0:T(8,128)(2,1)S(1)}, bf16[113,8,128]{2,1,0:T(8,128)(2,1)S(1)}, u32[]{:S(2)}, u32[]{:S(2)}) collective-permute-start(bf16[113,8,128]{2,1,0:T(8,128)(2,1)S(1)} %get-tuple-element.66), channel_id=1, source_target_pairs={{0,2},{1,3},{2,0},{3,1},{4,6},{5,7},{6,4},{7,5},{8,10},{9,11},{10,... | collective-permute-start | bytes 694280 | tf_op jit(solution)/shard_map/ppermute | solution.py:335
  103.7 6.6 %features.7 = (bf16[113,8,128]{2,1,0:T(8,128)(2,1)}, bf16[113,8,128]{2,1,0:T(8,128)(2,1)}, bf16[113,8,128]{2,1,0:T(8,128)(2,1)}, bf16[113,8,128]{2,1,0:T(8,128)(2,1)}) custom-call(bf16[7,64,128]{2,1,0:T(8,128)(2,1)S(1)} %bitcast.23, bf16[7,64,128]{2,1,0:T(8,128)(2,1)S(1)} %bitcast.24, bf16[7,64,128]{2,1,0:T(8,128)(2,1)S(1)} %bitcast.25, ...), custom_call_target="tpu_custom_call" | custom-call | flops 2818572288 | bytes 7340032 | tf_op jit(solution)/shard_map/features/pallas_call | solution.py:382
  110.3 9.6 %collective-permute-done.30.refs_15_ = bf16[113,8,128]{2,1,0:T(8,128)(2,1)S(1)} collective-permute-done((bf16[113,8,128]{2,1,0:T(8,128)(2,1)S(1)}, bf16[113,8,128]{2,1,0:T(8,128)(2,1)S(1)}, u32[]{:S(2)}, u32[]{:S(2)}) %collective-permute-start.30) | collective-permute-done | bytes 231456 | tf_op jit(solution)/shard_map/ppermute | solution.py:335
  121.3 2.1 %collective-permute-start.17 = (bf16[113,8,128]{2,1,0:T(8,128)(2,1)}, bf16[113,8,128]{2,1,0:T(8,128)(2,1)S(1)}, u32[]{:S(2)}, u32[]{:S(2)}) collective-permute-start(bf16[113,8,128]{2,1,0:T(8,128)(2,1)} %get-tuple-element.62), channel_id=1, source_target_pairs={{0,13},{1,12},{2,15},{3,14},{4,9},{5,8},{6,11},{7,10},{8,5},{9,4},... | collective-permute-start | bytes 694280 | tf_op jit(solution)/shard_map/ppermute | solution.py:335
  134.9 6.7 %combine.2 = (f32[32,8,3584]{2,1,0:T(8,128)S(1)}, f32[32,8,3584]{2,1,0:T(8,128)S(1)}, f32[32,8,128]{2,1,0:T(8,128)S(1)}) custom-call(s32[1]{0:T(128)} %bitcast.refs_0_.refs_9_, s32[64]{0:T(128)S(1)} %reshape.101.refs_2_.refs_1_, s32[112]{0:T(128)S(1)} %reshape.102.refs_3_.refs_2_, s32[112]{0:T(128)S(1)} %reshape.103.refs_3_, ...), custom_call_target="tpu_custom_call" | custom-call | flops 10000000 | bytes 10000000 | tf_op jit(solution)/shard_map/combine/pallas_call | solution.py:396
  141.5 5.9 %collective-permute-done.16.refs_4_ = bf16[113,8,128]{2,1,0:T(8,128)(2,1)S(1)} collective-permute-done((bf16[113,8,128]{2,1,0:T(8,128)(2,1)}, bf16[113,8,128]{2,1,0:T(8,128)(2,1)S(1)}, u32[]{:S(2)}, u32[]{:S(2)}) %collective-permute-start.16) | collective-permute-done | bytes 231456 | tf_op jit(solution)/shard_map/ppermute | solution.py:335
  147.4 6.6 %collective-permute-done.17.refs_5_ = bf16[113,8,128]{2,1,0:T(8,128)(2,1)S(1)} collective-permute-done((bf16[113,8,128]{2,1,0:T(8,128)(2,1)}, bf16[113,8,128]{2,1,0:T(8,128)(2,1)S(1)}, u32[]{:S(2)}, u32[]{:S(2)}) %collective-permute-start.17) | collective-permute-done | bytes 231456 | tf_op jit(solution)/shard_map/ppermute | solution.py:335
  154.0 3.4 %collective-permute-done.18.refs_6_ = bf16[113,8,128]{2,1,0:T(8,128)(2,1)S(1)} collective-permute-done((bf16[113,8,128]{2,1,0:T(8,128)(2,1)}, bf16[113,8,128]{2,1,0:T(8,128)(2,1)S(1)}, u32[]{:S(2)}, u32[]{:S(2)}) %collective-permute-start.18) | collective-permute-done | bytes 231456 | tf_op jit(solution)/shard_map/ppermute | solution.py:335
  157.4 5.6 %collective-permute-done.19.refs_7_ = bf16[113,8,128]{2,1,0:T(8,128)(2,1)S(1)} collective-permute-done((bf16[113,8,128]{2,1,0:T(8,128)(2,1)}, bf16[113,8,128]{2,1,0:T(8,128)(2,1)S(1)}, u32[]{:S(2)}, u32[]{:S(2)}) %collective-permute-start.19) | collective-permute-done | bytes 231456 | tf_op jit(solution)/shard_map/ppermute | solution.py:335
  163.0 5.4 %combine.3 = (bf16[32,8,3584]{2,1,0:T(8,128)(2,1)}, bf16[32,8,3584]{2,1,0:T(8,128)(2,1)}, f32[2,128]{1,0:T(2,128)}, f32[32,8,3584]{2,1,0:T(8,128)S(1)}, f32[32,8...) custom-call(s32[1]{0:T(128)} %bitcast.refs_0_.refs_9_, ...), custom_call_target="tpu_custom_call", output_to_operand_aliasing={{3}: (8, {}), {4}: (9, {}), {5}: (10, {})} | custom-call | flops 10000000 | bytes 10000000 | tf_op jit(solution)/shard_map/combine/pallas_call | solution.py:396
  (97 shorter events, 32.4 us)
Async XLA Ops:
  1.9 14.0 %collective-permute-start = (bf16[128,3584]{1,0:T(8,128)(2,1)S(1)}, bf16[128,3584]{1,0:T(8,128)(2,1)S(1)}, u32[]{:S(2)}, u32[]{:S(2)}) collective-permute-start(bf16[128,3584]{1,0:T(8,128)(2,1)S(1)} %slice.3), channel_id=1, source_target_pairs={{0,1},{1,2},{2,3},{3,4},{4,5},{5,6},{6,7},{7,8},{8,9},{9,10},{10,1... | collective-permute-start | bytes 2752520 | tf_op jit(solution)/shard_map/ppermute | solution.py:298
  9.6 37.9 %copy-start.19 = (bf16[2048,896]{1,0:T(8,128)(2,1)S(1)}, bf16[2048,896]{1,0:T(8,128)(2,1)}, u32[]{:S(2)}) copy-start(bf16[2048,896]{1,0:T(8,128)(2,1)} %refs_5_.7) | copy-start | bytes 11010052
  22.1 8.1 %collective-permute-start.1 = (bf16[7,8,8,128]{3,2,1,0:T(8,128)(2,1)S(1)}, bf16[7,8,8,128]{3,2,1,0:T(8,128)(2,1)S(1)}, u32[]{:S(2)}, u32[]{:S(2)}) collective-permute-start(bf16[7,8,8,128]{3,2,1,0:T(8,128)(2,1)S(1)} %get-tuple-element.42), channel_id=1, source_target_pairs={{0,12},{1,13},{2,14},{3,15},{4,8},{5,9},{6,10},{7,11},{8,4},{9,5},... | collective-permute-start | bytes 344072 | tf_op jit(solution)/shard_map/ppermute | solution.py:335
  22.7 12.0 %collective-permute-start.2 = (bf16[7,8,8,128]{3,2,1,0:T(8,128)(2,1)S(1)}, bf16[7,8,8,128]{3,2,1,0:T(8,128)(2,1)S(1)}, u32[]{:S(2)}, u32[]{:S(2)}) collective-permute-start(bf16[7,8,8,128]{3,2,1,0:T(8,128)(2,1)S(1)} %get-tuple-element.43), channel_id=1, source_target_pairs={{0,13},{1,12},{2,15},{3,14},{4,9},{5,8},{6,11},{7,10},{8,5},{9,4},... | collective-permute-start | bytes 344072 | tf_op jit(solution)/shard_map/ppermute | solution.py:335
  24.6 11.7 %collective-permute-start.12 = (bf16[7,8,8,128]{3,2,1,0:T(8,128)(2,1)S(1)}, bf16[7,8,8,128]{3,2,1,0:T(8,128)(2,1)S(1)}, u32[]{:S(2)}, u32[]{:S(2)}) collective-permute-start(bf16[7,8,8,128]{3,2,1,0:T(8,128)(2,1)S(1)} %get-tuple-element.54), channel_id=1, source_target_pairs={{0,4},{1,5},{2,6},{3,7},{4,0},{5,1},{6,2},{7,3},{8,12},{9,13},{10,... | collective-permute-start | bytes 344072 | tf_op jit(solution)/shard_map/ppermute | solution.py:335
  27.1 11.5 %collective-permute-start.13 = (bf16[7,8,8,128]{3,2,1,0:T(8,128)(2,1)S(1)}, bf16[7,8,8,128]{3,2,1,0:T(8,128)(2,1)S(1)}, u32[]{:S(2)}, u32[]{:S(2)}) collective-permute-start(bf16[7,8,8,128]{3,2,1,0:T(8,128)(2,1)S(1)} %get-tuple-element.55), channel_id=1, source_target_pairs={{0,5},{1,4},{2,7},{3,6},{4,1},{5,0},{6,3},{7,2},{8,13},{9,12},{10,... | collective-permute-start | bytes 344072 | tf_op jit(solution)/shard_map/ppermute | solution.py:335
  27.2 12.1 %collective-permute-start.14 = (bf16[7,8,8,128]{3,2,1,0:T(8,128)(2,1)S(1)}, bf16[7,8,8,128]{3,2,1,0:T(8,128)(2,1)S(1)}, u32[]{:S(2)}, u32[]{:S(2)}) collective-permute-start(bf16[7,8,8,128]{3,2,1,0:T(8,128)(2,1)S(1)} %get-tuple-element.56), channel_id=1, source_target_pairs={{0,6},{1,7},{2,4},{3,5},{4,2},{5,3},{6,0},{7,1},{8,14},{9,15},{10,... | collective-permute-start | bytes 344072 | tf_op jit(solution)/shard_map/ppermute | solution.py:335
  30.2 14.6 %collective-permute-start.15 = (bf16[7,8,8,128]{3,2,1,0:T(8,128)(2,1)S(1)}, bf16[7,8,8,128]{3,2,1,0:T(8,128)(2,1)S(1)}, u32[]{:S(2)}, u32[]{:S(2)}) collective-permute-start(bf16[7,8,8,128]{3,2,1,0:T(8,128)(2,1)S(1)} %get-tuple-element.57), channel_id=1, source_target_pairs={{0,7},{1,6},{2,5},{3,4},{4,3},{5,2},{6,1},{7,0},{8,15},{9,14},{10,... | collective-permute-start | bytes 344072 | tf_op jit(solution)/shard_map/ppermute | solution.py:335
  34.7 18.5 %collective-permute-start.3 = (bf16[7,8,8,128]{3,2,1,0:T(8,128)(2,1)S(1)}, bf16[7,8,8,128]{3,2,1,0:T(8,128)(2,1)S(1)}, u32[]{:S(2)}, u32[]{:S(2)}) collective-permute-start(bf16[7,8,8,128]{3,2,1,0:T(8,128)(2,1)S(1)} %get-tuple-element.44), channel_id=1, source_target_pairs={{0,14},{1,15},{2,12},{3,13},{4,10},{5,11},{6,8},{7,9},{8,6},{9,7},... | collective-permute-start | bytes 344072 | tf_op jit(solution)/shard_map/ppermute | solution.py:335
  36.3 18.4 %collective-permute-start.8 = (bf16[7,8,8,128]{3,2,1,0:T(8,128)(2,1)S(1)}, bf16[7,8,8,128]{3,2,1,0:T(8,128)(2,1)S(1)}, u32[]{:S(2)}, u32[]{:S(2)}) collective-permute-start(bf16[7,8,8,128]{3,2,1,0:T(8,128)(2,1)S(1)} %get-tuple-element.50), channel_id=1, source_target_pairs={{0,8},{1,9},{2,10},{3,11},{4,12},{5,13},{6,14},{7,15},{8,0},{9,1},... | collective-permute-start | bytes 344072 | tf_op jit(solution)/shard_map/ppermute | solution.py:335
  38.6 21.1 %collective-permute-start.9 = (bf16[7,8,8,128]{3,2,1,0:T(8,128)(2,1)S(1)}, bf16[7,8,8,128]{3,2,1,0:T(8,128)(2,1)S(1)}, u32[]{:S(2)}, u32[]{:S(2)}) collective-permute-start(bf16[7,8,8,128]{3,2,1,0:T(8,128)(2,1)S(1)} %get-tuple-element.51), channel_id=1, source_target_pairs={{0,9},{1,8},{2,11},{3,10},{4,13},{5,12},{6,15},{7,14},{8,1},{9,0},... | collective-permute-start | bytes 344072 | tf_op jit(solution)/shard_map/ppermute | solution.py:335
  39.3 22.9 %collective-permute-start.10 = (bf16[7,8,8,128]{3,2,1,0:T(8,128)(2,1)S(1)}, bf16[7,8,8,128]{3,2,1,0:T(8,128)(2,1)S(1)}, u32[]{:S(2)}, u32[]{:S(2)}) collective-permute-start(bf16[7,8,8,128]{3,2,1,0:T(8,128)(2,1)S(1)} %get-tuple-element.52), channel_id=1, source_target_pairs={{0,10},{1,11},{2,8},{3,9},{4,14},{5,15},{6,12},{7,13},{8,2},{9,3},... | collective-permute-start | bytes 344072 | tf_op jit(solution)/shard_map/ppermute | solution.py:335
  44.7 19.9 %collective-permute-start.11 = (bf16[7,8,8,128]{3,2,1,0:T(8,128)(2,1)S(1)}, bf16[7,8,8,128]{3,2,1,0:T(8,128)(2,1)S(1)}, u32[]{:S(2)}, u32[]{:S(2)}) collective-permute-start(bf16[7,8,8,128]{3,2,1,0:T(8,128)(2,1)S(1)} %get-tuple-element.53), channel_id=1, source_target_pairs={{0,11},{1,10},{2,9},{3,8},{4,15},{5,14},{6,13},{7,12},{8,3},{9,2},... | collective-permute-start | bytes 344072 | tf_op jit(solution)/shard_map/ppermute | solution.py:335
  53.2 20.5 %collective-permute-start.4 = (bf16[7,8,8,128]{3,2,1,0:T(8,128)(2,1)S(1)}, bf16[7,8,8,128]{3,2,1,0:T(8,128)(2,1)S(1)}, u32[]{:S(2)}, u32[]{:S(2)}) collective-permute-start(bf16[7,8,8,128]{3,2,1,0:T(8,128)(2,1)S(1)} %get-tuple-element.45), channel_id=1, source_target_pairs={{0,15},{1,14},{2,13},{3,12},{4,11},{5,10},{6,9},{7,8},{8,7},{9,6},... | collective-permute-start | bytes 344072 | tf_op jit(solution)/shard_map/ppermute | solution.py:335
  54.7 19.0 %collective-permute-start.5 = (bf16[7,8,8,128]{3,2,1,0:T(8,128)(2,1)S(1)}, bf16[7,8,8,128]{3,2,1,0:T(8,128)(2,1)S(1)}, u32[]{:S(2)}, u32[]{:S(2)}) collective-permute-start(bf16[7,8,8,128]{3,2,1,0:T(8,128)(2,1)S(1)} %get-tuple-element.47), channel_id=1, source_target_pairs={{0,1},{1,0},{2,3},{3,2},{4,5},{5,4},{6,7},{7,6},{8,9},{9,8},{10,11... | collective-permute-start | bytes 344072 | tf_op jit(solution)/shard_map/ppermute | solution.py:335
  59.8 15.5 %collective-permute-start.6 = (bf16[7,8,8,128]{3,2,1,0:T(8,128)(2,1)S(1)}, bf16[7,8,8,128]{3,2,1,0:T(8,128)(2,1)S(1)}, u32[]{:S(2)}, u32[]{:S(2)}) collective-permute-start(bf16[7,8,8,128]{3,2,1,0:T(8,128)(2,1)S(1)} %get-tuple-element.48), channel_id=1, source_target_pairs={{0,2},{1,3},{2,0},{3,1},{4,6},{5,7},{6,4},{7,5},{8,10},{9,11},{10,... | collective-permute-start | bytes 344072 | tf_op jit(solution)/shard_map/ppermute | solution.py:335
  62.2 14.4 %collective-permute-start.7 = (bf16[7,8,8,128]{3,2,1,0:T(8,128)(2,1)S(1)}, bf16[7,8,8,128]{3,2,1,0:T(8,128)(2,1)S(1)}, u32[]{:S(2)}, u32[]{:S(2)}) collective-permute-start(bf16[7,8,8,128]{3,2,1,0:T(8,128)(2,1)S(1)} %get-tuple-element.49), channel_id=1, source_target_pairs={{0,3},{1,2},{2,1},{3,0},{4,7},{5,6},{6,5},{7,4},{8,11},{9,10},{10,... | collective-permute-start | bytes 344072 | tf_op jit(solution)/shard_map/ppermute | solution.py:335
  64.7 12.1 %collective-permute-start.24 = (bf16[113,8,128]{2,1,0:T(8,128)(2,1)S(1)}, bf16[113,8,128]{2,1,0:T(8,128)(2,1)S(1)}, u32[]{:S(2)}, u32[]{:S(2)}) collective-permute-start(bf16[113,8,128]{2,1,0:T(8,128)(2,1)S(1)} %get-tuple-element.68), channel_id=1, source_target_pairs={{0,5},{1,4},{2,7},{3,6},{4,1},{5,0},{6,3},{7,2},{8,13},{9,12},{10,... | collective-permute-start | bytes 694280 | tf_op jit(solution)/shard_map/ppermute | solution.py:335
  73.6 27.2 %collective-permute-start.23 = (bf16[113,8,128]{2,1,0:T(8,128)(2,1)S(1)}, bf16[113,8,128]{2,1,0:T(8,128)(2,1)S(1)}, u32[]{:S(2)}, u32[]{:S(2)}) collective-permute-start(bf16[113,8,128]{2,1,0:T(8,128)(2,1)S(1)} %get-tuple-element.58.refs_9_), channel_id=1, source_target_pairs={{0,4},{1,5},{2,6},{3,7},{4,0},{5,1},{6,2},{7,3},{8,12},{9,13},{10,... | collective-permute-start | bytes 694280 | tf_op jit(solution)/shard_map/ppermute | solution.py:335
  73.7 19.8 %collective-permute-start.25 = (bf16[113,8,128]{2,1,0:T(8,128)(2,1)S(1)}, bf16[113,8,128]{2,1,0:T(8,128)(2,1)S(1)}, u32[]{:S(2)}, u32[]{:S(2)}) collective-permute-start(bf16[113,8,128]{2,1,0:T(8,128)(2,1)S(1)} %get-tuple-element.69), channel_id=1, source_target_pairs={{0,6},{1,7},{2,4},{3,5},{4,2},{5,3},{6,0},{7,1},{8,14},{9,15},{10,... | collective-permute-start | bytes 694280 | tf_op jit(solution)/shard_map/ppermute | solution.py:335
  75.3 23.2 %collective-permute-start.26 = (bf16[113,8,128]{2,1,0:T(8,128)(2,1)S(1)}, bf16[113,8,128]{2,1,0:T(8,128)(2,1)S(1)}, u32[]{:S(2)}, u32[]{:S(2)}) collective-permute-start(bf16[113,8,128]{2,1,0:T(8,128)(2,1)S(1)} %get-tuple-element.70), channel_id=1, source_target_pairs={{0,7},{1,6},{2,5},{3,4},{4,3},{5,2},{6,1},{7,0},{8,15},{9,14},{10,... | collective-permute-start | bytes 694280 | tf_op jit(solution)/shard_map/ppermute | solution.py:335
  76.7 24.6 %collective-permute-start.28 = (bf16[113,8,128]{2,1,0:T(8,128)(2,1)S(1)}, bf16[113,8,128]{2,1,0:T(8,128)(2,1)S(1)}, u32[]{:S(2)}, u32[]{:S(2)}) collective-permute-start(bf16[113,8,128]{2,1,0:T(8,128)(2,1)S(1)} %get-tuple-element.71), channel_id=1, source_target_pairs={{0,9},{1,8},{2,11},{3,10},{4,13},{5,12},{6,15},{7,14},{8,1},{9,0},... | collective-permute-start | bytes 694280 | tf_op jit(solution)/shard_map/ppermute | solution.py:335
  76.8 26.8 %collective-permute-start.29 = (bf16[113,8,128]{2,1,0:T(8,128)(2,1)S(1)}, bf16[113,8,128]{2,1,0:T(8,128)(2,1)S(1)}, u32[]{:S(2)}, u32[]{:S(2)}) collective-permute-start(bf16[113,8,128]{2,1,0:T(8,128)(2,1)S(1)} %get-tuple-element.72), channel_id=1, source_target_pairs={{0,10},{1,11},{2,8},{3,9},{4,14},{5,15},{6,12},{7,13},{8,2},{9,3},... | collective-permute-start | bytes 694280 | tf_op jit(solution)/shard_map/ppermute | solution.py:335
  93.5 27.2 %collective-permute-start.27 = (bf16[113,8,128]{2,1,0:T(8,128)(2,1)S(1)}, bf16[113,8,128]{2,1,0:T(8,128)(2,1)S(1)}, u32[]{:S(2)}, u32[]{:S(2)}) collective-permute-start(bf16[113,8,128]{2,1,0:T(8,128)(2,1)S(1)} %get-tuple-element.59.refs_9_), channel_id=1, source_target_pairs={{0,8},{1,9},{2,10},{3,11},{4,12},{5,13},{6,14},{7,15},{8,0},{9,1},... | collective-permute-start | bytes 694280 | tf_op jit(solution)/shard_map/ppermute | solution.py:335
  98.5 21.5 %collective-permute-start.30 = (bf16[113,8,128]{2,1,0:T(8,128)(2,1)S(1)}, bf16[113,8,128]{2,1,0:T(8,128)(2,1)S(1)}, u32[]{:S(2)}, u32[]{:S(2)}) collective-permute-start(bf16[113,8,128]{2,1,0:T(8,128)(2,1)S(1)} %get-tuple-element.73), channel_id=1, source_target_pairs={{0,11},{1,10},{2,9},{3,8},{4,15},{5,14},{6,13},{7,12},{8,3},{9,2},... | collective-permute-start | bytes 694280 | tf_op jit(solution)/shard_map/ppermute | solution.py:335
  100.9 22.6 %collective-permute-start.20 = (bf16[113,8,128]{2,1,0:T(8,128)(2,1)S(1)}, bf16[113,8,128]{2,1,0:T(8,128)(2,1)S(1)}, u32[]{:S(2)}, u32[]{:S(2)}) collective-permute-start(bf16[113,8,128]{2,1,0:T(8,128)(2,1)S(1)} %get-tuple-element.65), channel_id=1, source_target_pairs={{0,1},{1,0},{2,3},{3,2},{4,5},{5,4},{6,7},{7,6},{8,9},{9,8},{10,11... | collective-permute-start | bytes 694280 | tf_op jit(solution)/shard_map/ppermute | solution.py:335
  101.3 23.5 %collective-permute-start.21 = (bf16[113,8,128]{2,1,0:T(8,128)(2,1)S(1)}, bf16[113,8,128]{2,1,0:T(8,128)(2,1)S(1)}, u32[]{:S(2)}, u32[]{:S(2)}) collective-permute-start(bf16[113,8,128]{2,1,0:T(8,128)(2,1)S(1)} %get-tuple-element.66), channel_id=1, source_target_pairs={{0,2},{1,3},{2,0},{3,1},{4,6},{5,7},{6,4},{7,5},{8,10},{9,11},{10,... | collective-permute-start | bytes 694280 | tf_op jit(solution)/shard_map/ppermute | solution.py:335
  103.6 23.7 %collective-permute-start.22 = (bf16[113,8,128]{2,1,0:T(8,128)(2,1)}, bf16[113,8,128]{2,1,0:T(8,128)(2,1)}, u32[]{:S(2)}, u32[]{:S(2)}) collective-permute-start(bf16[113,8,128]{2,1,0:T(8,128)(2,1)} %get-tuple-element.67), channel_id=1, source_target_pairs={{0,3},{1,2},{2,1},{3,0},{4,7},{5,6},{6,5},{7,4},{8,11},{9,10},{10,... | collective-permute-start | bytes 694280 | tf_op jit(solution)/shard_map/ppermute | solution.py:335
  120.6 26.8 %collective-permute-start.16 = (bf16[113,8,128]{2,1,0:T(8,128)(2,1)}, bf16[113,8,128]{2,1,0:T(8,128)(2,1)S(1)}, u32[]{:S(2)}, u32[]{:S(2)}) collective-permute-start(bf16[113,8,128]{2,1,0:T(8,128)(2,1)} %get-tuple-element.61), channel_id=1, source_target_pairs={{0,12},{1,13},{2,14},{3,15},{4,8},{5,9},{6,10},{7,11},{8,4},{9,5},... | collective-permute-start | bytes 694280 | tf_op jit(solution)/shard_map/ppermute | solution.py:335
  121.3 32.6 %collective-permute-start.17 = (bf16[113,8,128]{2,1,0:T(8,128)(2,1)}, bf16[113,8,128]{2,1,0:T(8,128)(2,1)S(1)}, u32[]{:S(2)}, u32[]{:S(2)}) collective-permute-start(bf16[113,8,128]{2,1,0:T(8,128)(2,1)} %get-tuple-element.62), channel_id=1, source_target_pairs={{0,13},{1,12},{2,15},{3,14},{4,9},{5,8},{6,11},{7,10},{8,5},{9,4},... | collective-permute-start | bytes 694280 | tf_op jit(solution)/shard_map/ppermute | solution.py:335
  124.2 33.2 %collective-permute-start.18 = (bf16[113,8,128]{2,1,0:T(8,128)(2,1)}, bf16[113,8,128]{2,1,0:T(8,128)(2,1)S(1)}, u32[]{:S(2)}, u32[]{:S(2)}) collective-permute-start(bf16[113,8,128]{2,1,0:T(8,128)(2,1)} %get-tuple-element.63), channel_id=1, source_target_pairs={{0,14},{1,15},{2,12},{3,13},{4,10},{5,11},{6,8},{7,9},{8,6},{9,7},... | collective-permute-start | bytes 694280 | tf_op jit(solution)/shard_map/ppermute | solution.py:335
  125.5 37.5 %collective-permute-start.19 = (bf16[113,8,128]{2,1,0:T(8,128)(2,1)}, bf16[113,8,128]{2,1,0:T(8,128)(2,1)S(1)}, u32[]{:S(2)}, u32[]{:S(2)}) collective-permute-start(bf16[113,8,128]{2,1,0:T(8,128)(2,1)} %get-tuple-element.64), channel_id=1, source_target_pairs={{0,15},{1,14},{2,13},{3,12},{4,11},{5,10},{6,9},{7,8},{8,7},{9,6},... | collective-permute-start | bytes 694280 | tf_op jit(solution)/shard_map/ppermute | solution.py:335
  (24 other events, 268.1 us)
